TPU v7x, 128 devices: a whole 4x4x4 slice. The times are simulated.
128 devices in a mesh: dp: 32 (over x, z, core), mp: 4 (over y).
Axes of the slice: x: 4, y: 4, z: 4, core: 2. Of those that a mesh axis runs over, the one named last changes fastest.
Arguments:
- queries: bfloat16 [4096, 4, 2560], P('dp', None, 'mp'), may hold values from -96 to 96
- new_keys: bfloat16 [4096, 4, 512], P('dp', None, 'mp'), may hold values from -4 to 4
- new_values: bfloat16 [4096, 4, 512], P('dp', None, 'mp'), may hold values from -12 to 12
- key_cache: bfloat16 [4096, 256, 512], P('dp', None, 'mp'), may hold values from -4 to 4
- value_cache: bfloat16 [4096, 256, 512], P('dp', None, 'mp'), may hold values from -12 to 12
- lengths: int32 [4096], P('dp'), may hold values from 1 to 256
- rewards: int32 [4096], P('dp'), may hold values from 0 to 4
- group_ids: int32 [4096], P('dp'), may hold values from 0 to 511, as said below
- destination: int32 [4096], P('dp'), may hold values from 0 to 4095, as said below
- out_proj: bfloat16 [5120, 2560], P('dp', 'mp'), may hold values from -0.125 to 0.125
- cotangent: bfloat16 [16384, 5120], P('dp', 'mp'), may hold values from -6 to 6
Outputs:
- out_y: bfloat16 [16384, 5120], P('dp', 'mp')
- grad_attn: bfloat16 [16384, 2560], P('dp', 'mp')
- grad_proj: bfloat16 [5120, 2560], P('dp', 'mp')
Inputs may be any that keep to these rules, and one draw needn't show every extreme that they name: `group_ids`: each group has exactly 8 responses. `destination`: a permutation of the 4096 positions; positions d * 128 to (d + 1) * 128 - 1 form block d; of the responses of one index of dp at most 8 go to any one block, and exactly 8 to some block.
All inputs are finite; a program needn't handle non-finite values.
Results may differ from a plain program's by a relative error of at most 0.015.
Values may be sent and summed in bfloat16 or wider, within the bound.
No kernel may reach another device: no remote copies, remote signals or barrier semaphores. Data moves between devices by JAX's collectives and lax.ppermute only.
A program may use at most 128 MiB of HBM per device.

v0:
```python
import functools

import jax
import jax.numpy as jnp
from jax import lax
from jax.experimental import pallas as pl
from jax.experimental.pallas import tpu as pltpu
from jax.sharding import PartitionSpec as P

HD = 128
G = 8
CAP = 8
NX, NZ, NY = 4, 4, 4
BF = jnp.bfloat16
F32 = jnp.float32


def place(x, z, c):
    return (x % NX) * 8 + (z % NZ) * 2 + c


def everywhere():
    return [(x, z, c) for x in range(NX) for z in range(NZ) for c in range(2)]


def along_x(value, shift):
    return lax.ppermute(
        value, "dp", [(place(x, z, c), place(x + shift, z, c)) for x, z, c in everywhere()]
    )


def along_z(value, shift):
    return lax.ppermute(
        value, "dp", [(place(x, z, c), place(x, z + shift, c)) for x, z, c in everywhere()]
    )


def along_y(value, shift):
    return lax.ppermute(value, "mp", [(y, (y + shift) % NY) for y in range(NY)])


def to_partner(value):
    return lax.ppermute(value, "dp", [(d, d ^ 1) for d in range(32)])


def swap_xy(value):
    pairs = [
        (place(x, z, c) * NY + y, place(y, z, c) * NY + x)
        for x, z, c in everywhere()
        for y in range(NY)
    ]
    return lax.ppermute(value, ("dp", "mp"), pairs)


def attend_kernel(
    lengths_ref, q_ref, nk_ref, nv_ref, k_ref, v_ref, out_ref, *, first
):
    rows, steps, _ = q_ref.shape
    cache = k_ref.shape[1]
    scale = HD ** (-0.5)
    base = (first + pl.program_id(0)) * rows
    q = q_ref[...].astype(F32)
    heads = [q[:, :, h * HD : (h + 1) * HD] for h in range(5)]
    heads.append(jnp.zeros_like(heads[0]))
    q = jnp.concatenate(
        [jnp.concatenate(heads[h : h + 2], axis=1) for h in (0, 2, 4)], axis=1
    ).astype(BF)
    width = q.shape[1]
    fresh = lax.dot_general(
        q.reshape(rows * width, HD),
        nk_ref[...],
        (((1,), (1,)), ((), ())),
        preferred_element_type=F32,
    )
    shape = (rows, width, rows * steps)
    col = lax.broadcasted_iota(jnp.int32, shape, 2)
    own = (col >> 2) == lax.broadcasted_iota(jnp.int32, shape, 0)
    causal = (col & 3) <= (lax.broadcasted_iota(jnp.int32, shape, 1) & 3)
    fresh = jnp.where(own & causal, fresh.reshape(shape), -jnp.inf)
    lane = lax.broadcasted_iota(jnp.int32, (width, cache), 1)
    past_weights, fresh_weights = [], []
    for r in range(rows):
        past = lax.dot_general(
            q[r], k_ref[r], (((1,), (1,)), ((), ())), preferred_element_type=F32
        )
        past = jnp.where(lane < lengths_ref[base + r], past, -jnp.inf)
        top = jnp.maximum(
            jnp.max(past, axis=-1, keepdims=True), jnp.max(fresh[r], axis=-1, keepdims=True)
        )
        past = jnp.exp((past - top) * scale)
        new = jnp.exp((fresh[r] - top) * scale)
        inverse = 1.0 / (
            jnp.sum(past, axis=-1, keepdims=True) + jnp.sum(new, axis=-1, keepdims=True)
        )
        past_weights.append((past * inverse).astype(BF))
        fresh_weights.append(new * inverse)
    fresh_weights = jnp.stack(fresh_weights, axis=0).reshape(rows * width, rows * steps)
    mixed = jnp.dot(fresh_weights.astype(BF), nv_ref[...], preferred_element_type=F32)
    mixed = mixed.reshape(rows, width, HD)
    got = [
        mixed[r] + jnp.dot(past_weights[r], v_ref[r], preferred_element_type=F32)
        for r in range(rows)
    ]
    for h in range(5):
        column = jnp.concatenate([g[h * steps : (h + 1) * steps] for g in got], axis=0)
        out_ref[:, h * HD : (h + 1) * HD] = column.astype(BF)


def attend(lengths, queries, fresh_keys, fresh_vals, key_cache, value_cache, first, count):
    rows = 8
    steps, width = queries.shape[1:]
    cache = key_cache.shape[1]
    first = first // rows
    cached = pl.BlockSpec((rows, cache, HD), lambda i, lens: (first + i, 0, 0))
    fresh = pl.BlockSpec((rows * steps, HD), lambda i, lens: (first + i, 0))
    return pl.pallas_call(
        functools.partial(attend_kernel, first=first),
        out_shape=jax.ShapeDtypeStruct((count * steps, width), BF),
        grid_spec=pltpu.PrefetchScalarGridSpec(
            num_scalar_prefetch=1,
            grid=(count // rows,),
            in_specs=[
                pl.BlockSpec((rows, steps, width), lambda i, lens: (first + i, 0, 0)),
                fresh,
                fresh,
                cached,
                cached,
            ],
            out_specs=pl.BlockSpec((rows * steps, width), lambda i, lens: (i, 0)),
        ),
        name="attend",
    )(lengths, queries, fresh_keys, fresh_vals, key_cache, value_cache)


def pack_kernel(goes_ref, facts_ref, a_ref, b_ref, out_ref):
    half = a_ref.shape[0]
    blocks = 8

    @pl.loop(0, out_ref.shape[0] // blocks)
    def _(k):
        size = blocks * 32
        slot = lax.broadcasted_iota(jnp.int32, (size, 2 * half), 0) + k * size
        chosen = (slot == goes_ref[...]).astype(F32).astype(BF)
        got = jnp.dot(chosen[:, :half], a_ref[...], preferred_element_type=F32)
        got = got + jnp.dot(chosen[:, half:], b_ref[...], preferred_element_type=F32)
        got = got.astype(BF)
        for i in range(blocks):
            out_ref[k * blocks + i, :32] = got[i * 32 : (i + 1) * 32]
            out_ref[k * blocks + i, 32:] = facts_ref[...]


def pack(goes_to, facts, first, second):
    return pl.pallas_call(
        pack_kernel,
        out_shape=jax.ShapeDtypeStruct((32, 40, first.shape[1]), BF),
        in_specs=[pl.BlockSpec(memory_space=pltpu.VMEM)] * 4,
        out_specs=pl.BlockSpec(memory_space=pltpu.VMEM),
        name="pack",
    )(goes_to, facts, first, second)


def unpack_kernel(block_ref, facts_ref, rows_ref, acts_ref, word_ref):
    tokens = acts_ref.shape[0]
    lanes = facts_ref.shape[2]
    token = lax.broadcasted_iota(jnp.int32, (tokens, lanes), 0)
    wanted = (token >> 2) + block_ref[0] * 128

    def look(k, found):
        fact = facts_ref[k].astype(F32).astype(jnp.int32)
        spot = fact[0:1] + 128 * fact[1:2]
        group = fact[2:3] * 16 + fact[3:4]
        word = group + fact[4:5] * 512 + (fact[5:6] * 4 + k * 40) * 4096
        return found + jnp.where(spot == wanted, word, 0)

    found = lax.fori_loop(0, facts_ref.shape[0], look, jnp.zeros((tokens, lanes), jnp.int32))
    found = jnp.sum(found, axis=1, keepdims=True)
    word_ref[...] = found
    total_rows = rows_ref.shape[0]
    source = (found >> 12) + (lax.broadcasted_iota(jnp.int32, (tokens, 1), 0) & 3)
    column = lax.broadcasted_iota(jnp.int32, (tokens, total_rows), 1)
    chosen = (column == source).astype(F32).astype(BF)
    acts_ref[...] = jnp.dot(chosen, rows_ref[...], preferred_element_type=F32).astype(BF)


def unpack(block, got):
    width = got.shape[2]
    return pl.pallas_call(
        unpack_kernel,
        out_shape=(
            jax.ShapeDtypeStruct((512, width), BF),
            jax.ShapeDtypeStruct((512, 1), jnp.int32),
        ),
        grid=(1,),
        in_specs=[
            pl.BlockSpec(memory_space=pltpu.SMEM),
            pl.BlockSpec((32, 8, 128), lambda i: (0, 4, 0)),
            pl.BlockSpec((32 * 40, width), lambda i: (0, 0)),
        ],
        out_specs=(
            pl.BlockSpec((512, width), lambda i: (0, 0)),
            pl.BlockSpec((512, 1), lambda i: (0, 0)),
        ),
        name="unpack",
    )(block, got, got.reshape(32 * 40, width))


def signal_kernel(facts_ref, word_ref, cot_ref, out_ref):
    tokens = out_ref.shape[0]
    lanes = facts_ref.shape[2]
    group = word_ref[...] & 511

    def add(k, sums):
        fact = facts_ref[k].astype(F32).astype(jnp.int32)
        reward = fact[4:5]
        word = reward + reward * reward * 4096
        return sums + jnp.where(fact[2:3] * 16 + fact[3:4] == group, word, 0)

    sums = lax.fori_loop(0, facts_ref.shape[0], add, jnp.zeros((tokens, lanes), jnp.int32))
    sums = jnp.sum(sums, axis=1, keepdims=True)
    centre = (sums & 4095).astype(F32) / G
    spread = (sums >> 12).astype(F32) / G - centre * centre
    reward = ((word_ref[...] >> 9) & 7).astype(F32)
    advantage = (reward - centre) / jnp.sqrt(jnp.maximum(spread, 1.0))
    out_ref[...] = (advantage * cot_ref[...].astype(F32)).astype(BF)


def weigh(got, word, cotangent):
    whole = lambda a: pl.BlockSpec(a.shape, lambda i: (0, 0))
    return pl.pallas_call(
        signal_kernel,
        out_shape=jax.ShapeDtypeStruct(cotangent.shape, BF),
        grid=(1,),
        in_specs=[
            pl.BlockSpec((32, 8, 128), lambda i: (0, 4, 0)),
            whole(word),
            whole(cotangent),
        ],
        out_specs=whole(cotangent),
        name="weigh",
    )(got, word, cotangent)


def grad_kernel(where_ref, left_ref, *refs):
    mine, theirs, (a_ref, b_ref) = refs[:4], refs[4:8], refs[8:]
    tokens = mine[0].shape[0]
    x, z, y = where_ref[0], where_ref[1], where_ref[2]
    half = left_ref.shape[0] // 2
    step = half // NZ
    for i in range(NY):
        xs = lax.rem(y - i - x + 2 * NX, NX)
        left = left_ref[...]
        got = jnp.dot(left[:, :tokens], mine[i][...], preferred_element_type=F32)
        got = got + jnp.dot(left[:, tokens:], theirs[i][...], preferred_element_type=F32)
        got = got.astype(BF)
        for k in range(NZ):
            zs = lax.rem(k - z + NZ, NZ)
            a_ref[xs, zs] = got[k * step : (k + 1) * step]
            b_ref[zs, xs] = got[half + k * step : half + (k + 1) * step]


def grad_parts(where, left, mine, theirs):
    width = mine[0].shape[1]
    step = left.shape[0] // 2 // NZ
    shape = jax.ShapeDtypeStruct((4, 4, step, width), BF)
    return pl.pallas_call(
        grad_kernel,
        out_shape=(shape, shape),
        in_specs=[pl.BlockSpec(memory_space=pltpu.SMEM)]
        + [pl.BlockSpec(memory_space=pltpu.VMEM)] * 9,
        out_specs=(
            pl.BlockSpec(memory_space=pltpu.VMEM),
            pl.BlockSpec(memory_space=pltpu.VMEM),
        ),
        name="grad_parts",
    )(where, left, *mine, *theirs)


def total(*parts):
    result = parts[0].astype(F32)
    for part in parts[1:]:
        result = result + part.astype(F32)
    return result


def local(
    queries,
    new_keys,
    new_values,
    key_cache,
    value_cache,
    lengths,
    rewards,
    group_ids,
    destination,
    out_proj,
    cotangent,
):
    row_count, step_count, feat_width = queries.shape
    tokens = row_count * step_count
    block = lax.axis_index("dp").astype(jnp.int32)
    y = lax.axis_index("mp").astype(jnp.int32)
    x, z, c = block // 8, (block // 2) % 4, block % 2

    weight_tile = swap_xy(out_proj)

    target = destination // row_count
    positions = jnp.arange(row_count, dtype=jnp.int32)
    earlier = (target[:, None] == target[None, :]) & (positions[None, :] < positions[:, None])
    rank = jnp.sum(earlier.astype(jnp.int32), axis=1)
    facts = jnp.stack(
        [destination % row_count, target, group_ids // 16, group_ids % 16, rewards, rank]
    )
    facts = jnp.pad(facts, ((0, 2), (0, feat_width - row_count))).astype(F32).astype(BF)
    steps = jnp.arange(step_count, dtype=jnp.int32)
    goes_to = ((target * CAP + rank)[:, None] * step_count + steps[None, :]).reshape(1, tokens)

    fresh_keys = new_keys.reshape(tokens, HD)
    fresh_vals = new_values.reshape(tokens, HD)
    half = row_count // 2
    caches = (fresh_keys, fresh_vals, key_cache, value_cache)
    first = attend(lengths, queries, *caches, 0, half)
    lengths, first, weight_tile = lax.optimization_barrier((lengths, first, weight_tile))
    second = attend(lengths, queries, *caches, half, half)
    weight = lax.all_gather(weight_tile, "dp", axis=0, tiled=True)
    weight = weight.reshape(NX, -1, feat_width)

    send_rows = pack(goes_to, facts, first, second)
    got_rows = lax.all_to_all(send_rows, "dp", split_axis=0, concat_axis=0, tiled=True)
    acts, word = unpack(block[None], got_rows)

    mine = [acts] + [along_y(acts, s) for s in (1, 2, 3)]
    theirs = [to_partner(block_cols) for block_cols in mine]

    signal = weigh(got_rows, word, cotangent)
    turned = signal.T.reshape(NZ, 2, 2, -1, tokens)
    sides = jnp.transpose(turned, (1, 2, 0, 3, 4)).reshape(2, -1, tokens)
    own_side = lax.dynamic_index_in_dim(sides, c, 0, keepdims=False)
    other_side = lax.dynamic_index_in_dim(sides, 1 - c, 0, keepdims=False)
    left = jnp.concatenate([own_side, to_partner(other_side)], axis=1)

    where = jnp.stack([x, z, y])
    part_a, part_b = grad_parts(where, left, mine, theirs)
    more_a = [along_x(part_a[s], s) for s in (1, 3, 2)]
    more_b = [along_z(part_b[s], s) for s in (1, 3, 2)]

    def columns(index):
        return lax.dynamic_index_in_dim(weight, index % NY, 0, keepdims=False)

    signal, _ = lax.optimization_barrier((signal, part_a))
    grad_blocks = [
        jnp.dot(signal, columns(y + s), preferred_element_type=F32).astype(BF) for s in range(NY)
    ]
    more_a, more_b, grad_blocks = lax.optimization_barrier((more_a, more_b, grad_blocks))
    more_grad = [along_y(grad_blocks[s], s) for s in (1, 3, 2)]

    part_a = total(part_a[0], *more_a).astype(BF)
    part_b = total(part_b[0], *more_b).astype(BF)
    more_a = [along_z(part_a[s], s) for s in (1, 3, 2)]
    more_b = [along_x(part_b[s], s) for s in (1, 3, 2)]

    mine, _ = lax.optimization_barrier((mine, grad_blocks))
    out_y = jnp.zeros((tokens, cotangent.shape[1]), F32)
    for s in range(NY):
        out_y = out_y + lax.dot_general(
            mine[s],
            columns(y - s + NY),
            (((1,), (1,)), ((), ())),
            preferred_element_type=F32,
        )
    out_y = out_y.astype(BF)
    more_a, more_b, out_y = lax.optimization_barrier((more_a, more_b, out_y))
    sum_a = total(part_a[0], *more_a)
    sum_b = total(part_b[0], *more_b)
    piece = (jnp.concatenate([sum_a, sum_b], axis=0) / 32).astype(BF)
    grad_proj = swap_xy(piece)
    grad_attn = total(grad_blocks[0], *more_grad).astype(BF)
    return (out_y, grad_attn, grad_proj)


def solution(mesh):
    placed = (
        P("dp", None, "mp"),
        P("dp", None, "mp"),
        P("dp", None, "mp"),
        P("dp", None, "mp"),
        P("dp", None, "mp"),
        P("dp"),
        P("dp"),
        P("dp"),
        P("dp"),
        P("dp", "mp"),
        P("dp", "mp"),
    )
    return jax.shard_map(
        local,
        mesh=mesh,
        in_specs=placed,
        out_specs=(P("dp", "mp"), P("dp", "mp"), P("dp", "mp")),
        check_vma=False,
    )
```

profile of v0, /device:TPU:4, one launch (start us, length us, event | category | flops | bytes accessed | tf_op | source)
XLA Modules:
  0.0 223.9 jit_solution(7044043380502726398)
XLA Ops:
  7.2 5.0 %collective-permute-start = (bf16[160,640]{1,0:T(8,128)(2,1)}, bf16[160,640]{1,0:T(8,128)(2,1)S(1)}, u32[]{:S(2)}, u32[]{:S(2)}) collective-permute-start(bf16[160,640]{1,0:T(8,128)(2,1)} %param.20), channel_id=1, source_target_pairs={{0,0},{1,32},{2,64},{3,96},{4,4},{5,36},{6,68},{7,100},{8,8},{9,40... | collective-permute-start | bytes 614408 | tf_op jit(solution)/shard_map/ppermute | solution.py:52
  12.3 9.9 %attend.2.a_ref = bf16[256,640]{1,0:T(8,128)(2,1)} custom-call(s32[128]{0:T(128)} %lengths_ref.2, bf16[128,4,640]{2,1,0:T(4,128)(2,1)} %q_ref.3, bf16[512,128]{1,0:T(8,128)(2,1)} %bitcast.107, bf16[512,128]{1,0:T(8,128)(2,1)} %bitcast.109, bf16[128,256,128]{2,1,0:T(8,128)(2,1)} %k_ref.3, bf16[128,256,128]{2,1,0:T(8,128)(2,1)} %v_ref.3), custom_call_target="tpu_custom_call" | custom-call | tf_op jit(solution)/shard_map/attend/pallas_call | solution.py:116
  26.2 9.8 %attend.3.b_ref = bf16[256,640]{1,0:T(8,128)(2,1)} custom-call(s32[128]{0:T(128)} %lengths_ref.2, bf16[128,4,640]{2,1,0:T(4,128)(2,1)} %q_ref.3, bf16[512,128]{1,0:T(8,128)(2,1)} %bitcast.108, bf16[512,128]{1,0:T(8,128)(2,1)} %bitcast.110, bf16[128,256,128]{2,1,0:T(8,128)(2,1)} %k_ref.3, bf16[128,256,128]{2,1,0:T(8,128)(2,1)} %v_ref.3), custom_call_target="tpu_custom_call" | custom-call | tf_op jit(solution)/shard_map/attend/pallas_call | solution.py:116
  36.0 3.8 %pack.1 = bf16[32,40,640]{2,1,0:T(8,128)(2,1)} custom-call(s32[1,512]{1,0:T(1,128)} %add.177.goes_ref, bf16[8,640]{1,0:T(8,128)(2,1)} %convert_convert_fusion.facts_ref, bf16[256,640]{1,0:T(8,128)(2,1)} %attend.2.a_ref, bf16[256,640]{1,0:T(8,128)(2,1)} %attend.3.b_ref), custom_call_target="tpu_custom_call" | custom-call | tf_op jit(solution)/shard_map/pack/pallas_call | solution.py:153
  39.8 8.5 %all-to-all-start = ((bf16[32,40,640]{2,1,0:T(8,128)(2,1)}), bf16[32,40,640]{2,1,0:T(8,128)(2,1)S(1)}, u32[]{:S(2)}, u32[]{:S(2)}) async-start(bf16[32,40,640]{2,1,0:T(8,128)(2,1)} %pack.1), calls=%async_computation | async-start | bytes 3276800 | tf_op jit(solution)/shard_map/all_to_all | solution.py:328
  48.3 29.0 %all-to-all-done.facts_ref = bf16[32,40,640]{2,1,0:T(8,128)(2,1)S(1)} async-done(((bf16[32,40,640]{2,1,0:T(8,128)(2,1)}), bf16[32,40,640]{2,1,0:T(8,128)(2,1)S(1)}, u32[]{:S(2)}, u32[]{:S(2)}) %all-to-all-start) | async-done | bytes 1638432 | tf_op jit(solution)/shard_map/all_to_all | solution.py:328
  78.5 5.7 %unpack.1 = (bf16[512,640]{1,0:T(8,128)(2,1)}, s32[512,1]{1,0:T(8,128)}) custom-call(s32[1]{0:T(128)} %bitcast.11.block_ref, bf16[32,40,640]{2,1,0:T(8,128)(2,1)} %copy-done, bf16[1280,640]{1,0:T(8,128)(2,1)} %bitcast.103), custom_call_target="tpu_custom_call" | custom-call | tf_op jit(solution)/shard_map/unpack/pallas_call | solution.py:187
  86.2 7.7 %weigh.1 = bf16[512,1280]{1,0:T(8,128)(2,1)} custom-call(bf16[32,40,640]{2,1,0:T(8,128)(2,1)} %copy-done, s32[512,1]{1,0:T(8,128)} %get-tuple-element.34.word_ref, bf16[512,1280]{1,0:T(8,128)(2,1)} %cot_ref.1), custom_call_target="tpu_custom_call" | custom-call | tf_op jit(solution)/shard_map/weigh/pallas_call | solution.py:229
  100.7 2.9 %collective-permute-start.8 = (bf16[512,640]{1,0:T(8,128)(2,1)S(1)}, bf16[512,640]{1,0:T(8,128)(2,1)}, u32[]{:S(2)}, u32[]{:S(2)}) collective-permute-start(bf16[512,640]{1,0:T(8,128)(2,1)S(1)} %collective-permute-done.4.refs_3_), channel_id=1, source_target_pairs={{0,4},{4,0},{8,12},{12,8},{16,20},{20,16},{24,28},{28,24},{32,36},... | collective-permute-start | bytes 1966088 | tf_op jit(solution)/shard_map/ppermute | solution.py:43
  104.8 12.8 %collective-permute-done.2.refs_1_ = bf16[512,640]{1,0:T(8,128)(2,1)} collective-permute-done((bf16[512,640]{1,0:T(8,128)(2,1)}, bf16[512,640]{1,0:T(8,128)(2,1)}, u32[]{:S(2)}, u32[]{:S(2)}) %collective-permute-start.2) | collective-permute-done | bytes 655392 | tf_op jit(solution)/shard_map/ppermute | solution.py:39
  120.0 8.8 %grad_parts.1 = (bf16[4,4,80,640]{3,2,1,0:T(8,128)(2,1)}, bf16[4,4,80,640]{3,2,1,0:T(8,128)(2,1)}) custom-call(s32[3]{0:T(128)} %pad_add_fusion.where_ref, bf16[640,1024]{1,0:T(8,128)(2,1)} %pad_maximum_fusion.left_ref, bf16[512,640]{1,0:T(8,128)(2,1)} %get-tuple-element.50.refs_0_, bf16[512,640]{1,0:T(8,128)(2,1)} %collective-permute-done.2.refs_1_, ...), custom_call_target="tpu_custom_call" | custom-call | tf_op jit(solution)/shard_map/grad_parts/pallas_call | solution.py:265
  128.8 2.4 %slice_bitcast_fusion = (bf16[4,80,640]{2,1,0:T(8,128)(2,1)}, bf16[4,80,640]{2,1,0:T(8,128)(2,1)}, bf16[4,80,640]{2,1,0:T(8,128)(2,1)S(1)}) fusion(bf16[4,4,80,640]{3,2,1,0:T(8,128)(2,1)} %get-tuple-element.37), kind=kLoop, calls=%fused_computation.45 | loop fusion | bytes 2457600 | tf_op jit(solution)/shard_map/squeeze | solution.py:344
  132.4 3.2 %collective-permute-start.13 = (bf16[4,80,640]{2,1,0:T(8,128)(2,1)}, bf16[4,80,640]{2,1,0:T(8,128)(2,1)}, u32[]{:S(2)}, u32[]{:S(2)}) collective-permute-start(bf16[4,80,640]{2,1,0:T(8,128)(2,1)} %get-tuple-element.62), channel_id=1, source_target_pairs={{0,24},{4,28},{8,0},{12,4},{16,8},{20,12},{24,16},{28,20},{32,56},... | collective-permute-start | bytes 1228808 | tf_op jit(solution)/shard_map/ppermute | solution.py:33
  139.9 2.8 %fusion.26 = bf16[512,640]{1,0:T(8,128)(2,1)S(1)} fusion(bf16[512,1280]{1,0:T(8,128)(2,1)S(1)} %copy-done.1, bf16[4,1280,640]{2,1,0:T(8,128)(2,1)} %bitcast.111, s32[]{:T(128)S(6)} %select_n.99), kind=kOutput, calls=%fused_computation.27 | convolution fusion | flops 839188480 | bytes 3604484 | tf_op jit(solution)/shard_map/dot_general | solution.py:351
  142.6 2.7 %fusion.35 = bf16[512,640]{1,0:T(8,128)(2,1)S(1)} fusion(bf16[512,1280]{1,0:T(8,128)(2,1)S(1)} %copy-done.1, bf16[4,1280,640]{2,1,0:T(8,128)(2,1)} %bitcast.112, s32[]{:T(128)S(6)} %select_n.105), kind=kOutput, calls=%fused_computation.30 | convolution fusion | flops 839188480 | bytes 3604484 | tf_op jit(solution)/shard_map/dot_general | solution.py:351
  149.0 3.0 %collective-permute-done.13 = bf16[4,80,640]{2,1,0:T(8,128)(2,1)} collective-permute-done((bf16[4,80,640]{2,1,0:T(8,128)(2,1)}, bf16[4,80,640]{2,1,0:T(8,128)(2,1)}, u32[]{:S(2)}, u32[]{:S(2)}) %collective-permute-start.13) | collective-permute-done | bytes 409632 | tf_op jit(solution)/shard_map/ppermute | solution.py:33
  153.3 4.8 %collective-permute-done.10 = bf16[4,80,640]{2,1,0:T(8,128)(2,1)} collective-permute-done((bf16[4,80,640]{2,1,0:T(8,128)(2,1)}, bf16[4,80,640]{2,1,0:T(8,128)(2,1)}, u32[]{:S(2)}, u32[]{:S(2)}) %collective-permute-start.10) | collective-permute-done | bytes 409632 | tf_op jit(solution)/shard_map/ppermute | solution.py:27
  165.6 2.5 %collective-permute-start.16 = (bf16[80,640]{1,0:T(8,128)(2,1)S(1)}, bf16[80,640]{1,0:T(8,128)(2,1)S(1)}, u32[]{:S(2)}, u32[]{:S(2)}) collective-permute-start(bf16[80,640]{1,0:T(8,128)(2,1)S(1)} %get-tuple-element.73), channel_id=1, source_target_pairs={{0,24},{4,28},{8,0},{12,4},{16,8},{20,12},{24,16},{28,20},{32,56},... | collective-permute-start | bytes 307208 | tf_op jit(solution)/shard_map/ppermute | solution.py:33
  170.4 2.4 %fusion.8 = f32[512,1280]{1,0:T(8,128)S(1)} fusion(bf16[512,640]{1,0:T(8,128)(2,1)} %collective-permute-done.3.refs_2_, bf16[4,1280,640]{2,1,0:T(8,128)(2,1)S(1)} %bitcast.116, s32[]{:T(128)S(6)} %select_n.103), kind=kOutput, calls=%fused_computation.9 | convolution fusion | flops 838860800 | bytes 4915204 | tf_op jit(solution)/shard_map/dot_general | solution.py:364
  176.4 3.6 %collective-permute-start.23 = (bf16[512,640]{1,0:T(8,128)(2,1)S(1)}, bf16[512,640]{1,0:T(8,128)(2,1)S(1)}, u32[]{:S(2)}, u32[]{:S(2)}) collective-permute-start(bf16[512,640]{1,0:T(8,128)(2,1)S(1)} %fusion.32), channel_id=1, source_target_pairs={{0,2},{1,3},{2,0},{3,1},{4,6},{5,7},{6,4},{7,5},{8,10},{9,11},{10,... | collective-permute-start | bytes 1966088 | tf_op jit(solution)/shard_map/ppermute | solution.py:39
  180.2 5.5 %collective-permute-start.24 = (bf16[160,640]{1,0:T(8,128)(2,1)S(1)}, bf16[160,640]{1,0:T(8,128)(2,1)S(1)}, u32[]{:S(2)}, u32[]{:S(2)}) collective-permute-start(bf16[160,640]{1,0:T(8,128)(2,1)S(1)} %fusion.44), channel_id=1, source_target_pairs={{0,0},{1,32},{2,64},{3,96},{4,4},{5,36},{6,68},{7,100},{8,8},{9,40... | collective-permute-start | bytes 614408 | tf_op jit(solution)/shard_map/ppermute | solution.py:52
  185.7 8.0 %collective-permute-done.24 = bf16[160,640]{1,0:T(8,128)(2,1)S(1)} collective-permute-done((bf16[160,640]{1,0:T(8,128)(2,1)S(1)}, bf16[160,640]{1,0:T(8,128)(2,1)S(1)}, u32[]{:S(2)}, u32[]{:S(2)}) %collective-permute-start.24) | collective-permute-done | bytes 204832 | tf_op jit(solution)/shard_map/ppermute | solution.py:52
  193.8 2.7 %collective-permute-done.21 = bf16[512,640]{1,0:T(8,128)(2,1)S(1)} collective-permute-done((bf16[512,640]{1,0:T(8,128)(2,1)S(1)}, bf16[512,640]{1,0:T(8,128)(2,1)S(1)}, u32[]{:S(2)}, u32[]{:S(2)}) %collective-permute-start.21) | collective-permute-done | bytes 655392 | tf_op jit(solution)/shard_map/ppermute | solution.py:39
  196.4 18.8 %collective-permute-done.23 = bf16[512,640]{1,0:T(8,128)(2,1)S(1)} collective-permute-done((bf16[512,640]{1,0:T(8,128)(2,1)S(1)}, bf16[512,640]{1,0:T(8,128)(2,1)S(1)}, u32[]{:S(2)}, u32[]{:S(2)}) %collective-permute-start.23) | collective-permute-done | bytes 655392 | tf_op jit(solution)/shard_map/ppermute | solution.py:39
  (94 shorter events, 43.4 us)
Async XLA Ops:
  7.2 132.7 %all-gather.2.cloned.1.call-start = ((), (), s32[]{:S(2)}) async-start(), calls=%async_computation.1 | async-start | bytes 6758400 | tf_op jit(solution)/shard_map/all_gather | solution.py:324
  7.2 16.6 %collective-permute-start = (bf16[160,640]{1,0:T(8,128)(2,1)}, bf16[160,640]{1,0:T(8,128)(2,1)S(1)}, u32[]{:S(2)}, u32[]{:S(2)}) collective-permute-start(bf16[160,640]{1,0:T(8,128)(2,1)} %param.20), channel_id=1, source_target_pairs={{0,0},{1,32},{2,64},{3,96},{4,4},{5,36},{6,68},{7,100},{8,8},{9,40... | collective-permute-start | bytes 614408 | tf_op jit(solution)/shard_map/ppermute | solution.py:52
  39.8 37.4 %all-to-all-start = ((bf16[32,40,640]{2,1,0:T(8,128)(2,1)}), bf16[32,40,640]{2,1,0:T(8,128)(2,1)S(1)}, u32[]{:S(2)}, u32[]{:S(2)}) async-start(bf16[32,40,640]{2,1,0:T(8,128)(2,1)} %pack.1), calls=%async_computation | async-start | bytes 3276800 | tf_op jit(solution)/shard_map/all_to_all | solution.py:328
  84.2 16.5 %collective-permute-start.4 = (bf16[512,640]{1,0:T(8,128)(2,1)}, bf16[512,640]{1,0:T(8,128)(2,1)S(1)}, u32[]{:S(2)}, u32[]{:S(2)}) collective-permute-start(bf16[512,640]{1,0:T(8,128)(2,1)} %get-tuple-element.50.refs_0_), channel_id=1, source_target_pairs={{0,3},{1,0},{2,1},{3,2},{4,7},{5,4},{6,5},{7,6},{8,11},{9,8},{10,9... | collective-permute-start | bytes 1966088 | tf_op jit(solution)/shard_map/ppermute | solution.py:39
  84.2 19.4 %collective-permute-start.3 = (bf16[512,640]{1,0:T(8,128)(2,1)}, bf16[512,640]{1,0:T(8,128)(2,1)}, u32[]{:S(2)}, u32[]{:S(2)}) collective-permute-start(bf16[512,640]{1,0:T(8,128)(2,1)} %get-tuple-element.50.refs_0_), channel_id=1, source_target_pairs={{0,2},{1,3},{2,0},{3,1},{4,6},{5,7},{6,4},{7,5},{8,10},{9,11},{10,... | collective-permute-start | bytes 1966088 | tf_op jit(solution)/shard_map/ppermute | solution.py:39
  85.0 32.5 %collective-permute-start.2 = (bf16[512,640]{1,0:T(8,128)(2,1)}, bf16[512,640]{1,0:T(8,128)(2,1)}, u32[]{:S(2)}, u32[]{:S(2)}) collective-permute-start(bf16[512,640]{1,0:T(8,128)(2,1)} %get-tuple-element.50.refs_0_), channel_id=1, source_target_pairs={{0,1},{1,2},{2,3},{3,0},{4,5},{5,6},{6,7},{7,4},{8,9},{9,10},{10,1... | collective-permute-start | bytes 1966088 | tf_op jit(solution)/shard_map/ppermute | solution.py:39
  95.8 22.6 %collective-permute-start.1 = (bf16[640,512]{1,0:T(8,128)(2,1)S(1)}, bf16[640,512]{1,0:T(8,128)(2,1)S(1)}, u32[]{:S(2)}, u32[]{:S(2)}) collective-permute-start(bf16[640,512]{1,0:T(8,128)(2,1)S(1)} %get-tuple-element.68), channel_id=1, source_target_pairs={{0,4},{4,0},{8,12},{12,8},{16,20},{20,16},{24,28},{28,24},{32,36},... | collective-permute-start | bytes 1966088 | tf_op jit(solution)/shard_map/ppermute | solution.py:43
  97.5 22.1 %collective-permute-start.5 = (bf16[512,640]{1,0:T(8,128)(2,1)S(1)}, bf16[512,640]{1,0:T(8,128)(2,1)}, u32[]{:S(2)}, u32[]{:S(2)}) collective-permute-start(bf16[512,640]{1,0:T(8,128)(2,1)S(1)} %copy-done.2), channel_id=1, source_target_pairs={{0,4},{4,0},{8,12},{12,8},{16,20},{20,16},{24,28},{28,24},{32,36},... | collective-permute-start | bytes 1966088 | tf_op jit(solution)/shard_map/ppermute | solution.py:43
  100.7 19.0 %collective-permute-start.8 = (bf16[512,640]{1,0:T(8,128)(2,1)S(1)}, bf16[512,640]{1,0:T(8,128)(2,1)}, u32[]{:S(2)}, u32[]{:S(2)}) collective-permute-start(bf16[512,640]{1,0:T(8,128)(2,1)S(1)} %collective-permute-done.4.refs_3_), channel_id=1, source_target_pairs={{0,4},{4,0},{8,12},{12,8},{16,20},{20,16},{24,28},{28,24},{32,36},... | collective-permute-start | bytes 1966088 | tf_op jit(solution)/shard_map/ppermute | solution.py:43
  103.5 16.1 %collective-permute-start.7 = (bf16[512,640]{1,0:T(8,128)(2,1)}, bf16[512,640]{1,0:T(8,128)(2,1)}, u32[]{:S(2)}, u32[]{:S(2)}) collective-permute-start(bf16[512,640]{1,0:T(8,128)(2,1)} %collective-permute-done.3.refs_2_), channel_id=1, source_target_pairs={{0,4},{4,0},{8,12},{12,8},{16,20},{20,16},{24,28},{28,24},{32,36},... | collective-permute-start | bytes 1966088 | tf_op jit(solution)/shard_map/ppermute | solution.py:43
  131.2 14.2 %collective-permute-start.14 = (bf16[4,80,640]{2,1,0:T(8,128)(2,1)}, bf16[4,80,640]{2,1,0:T(8,128)(2,1)}, u32[]{:S(2)}, u32[]{:S(2)}) collective-permute-start(bf16[4,80,640]{2,1,0:T(8,128)(2,1)} %get-tuple-element.61), channel_id=1, source_target_pairs={{0,16},{4,20},{8,24},{12,28},{16,0},{20,4},{24,8},{28,12},{32,48},... | collective-permute-start | bytes 1228808 | tf_op jit(solution)/shard_map/ppermute | solution.py:33
  132.4 19.7 %collective-permute-start.13 = (bf16[4,80,640]{2,1,0:T(8,128)(2,1)}, bf16[4,80,640]{2,1,0:T(8,128)(2,1)}, u32[]{:S(2)}, u32[]{:S(2)}) collective-permute-start(bf16[4,80,640]{2,1,0:T(8,128)(2,1)} %get-tuple-element.62), channel_id=1, source_target_pairs={{0,24},{4,28},{8,0},{12,4},{16,8},{20,12},{24,16},{28,20},{32,56},... | collective-permute-start | bytes 1228808 | tf_op jit(solution)/shard_map/ppermute | solution.py:33
  135.6 17.7 %collective-permute-start.12 = (bf16[4,80,640]{2,1,0:T(8,128)(2,1)S(1)}, bf16[4,80,640]{2,1,0:T(8,128)(2,1)}, u32[]{:S(2)}, u32[]{:S(2)}) collective-permute-start(bf16[4,80,640]{2,1,0:T(8,128)(2,1)S(1)} %get-tuple-element.63), channel_id=1, source_target_pairs={{0,8},{4,12},{8,16},{12,20},{16,24},{20,28},{24,0},{28,4},{32,40},... | collective-permute-start | bytes 1228808 | tf_op jit(solution)/shard_map/ppermute | solution.py:33
  136.6 16.7 %collective-permute-start.11 = (bf16[4,80,640]{2,1,0:T(8,128)(2,1)}, bf16[4,80,640]{2,1,0:T(8,128)(2,1)}, u32[]{:S(2)}, u32[]{:S(2)}) collective-permute-start(bf16[4,80,640]{2,1,0:T(8,128)(2,1)} %get-tuple-element.64), channel_id=1, source_target_pairs={{0,64},{4,68},{8,72},{12,76},{16,80},{20,84},{24,88},{28,92},{32,9... | collective-permute-start | bytes 1228808 | tf_op jit(solution)/shard_map/ppermute | solution.py:27
  138.6 19.5 %collective-permute-start.10 = (bf16[4,80,640]{2,1,0:T(8,128)(2,1)}, bf16[4,80,640]{2,1,0:T(8,128)(2,1)}, u32[]{:S(2)}, u32[]{:S(2)}) collective-permute-start(bf16[4,80,640]{2,1,0:T(8,128)(2,1)} %get-tuple-element.65), channel_id=1, source_target_pairs={{0,96},{4,100},{8,104},{12,108},{16,112},{20,116},{24,120},{28,124... | collective-permute-start | bytes 1228808 | tf_op jit(solution)/shard_map/ppermute | solution.py:27
  160.2 13.8 %collective-permute-start.20 = (bf16[80,640]{1,0:T(8,128)(2,1)S(1)}, bf16[80,640]{1,0:T(8,128)(2,1)S(1)}, u32[]{:S(2)}, u32[]{:S(2)}) collective-permute-start(bf16[80,640]{1,0:T(8,128)(2,1)S(1)} %get-tuple-element.69), channel_id=1, source_target_pairs={{0,64},{4,68},{8,72},{12,76},{16,80},{20,84},{24,88},{28,92},{32,9... | collective-permute-start | bytes 307208 | tf_op jit(solution)/shard_map/ppermute | solution.py:27
  162.5 13.9 %collective-permute-start.19 = (bf16[80,640]{1,0:T(8,128)(2,1)S(1)}, bf16[80,640]{1,0:T(8,128)(2,1)S(1)}, u32[]{:S(2)}, u32[]{:S(2)}) collective-permute-start(bf16[80,640]{1,0:T(8,128)(2,1)S(1)} %get-tuple-element.70), channel_id=1, source_target_pairs={{0,96},{4,100},{8,104},{12,108},{16,112},{20,116},{24,120},{28,124... | collective-permute-start | bytes 307208 | tf_op jit(solution)/shard_map/ppermute | solution.py:27
  163.3 13.2 %collective-permute-start.18 = (bf16[80,640]{1,0:T(8,128)(2,1)S(1)}, bf16[80,640]{1,0:T(8,128)(2,1)S(1)}, u32[]{:S(2)}, u32[]{:S(2)}) collective-permute-start(bf16[80,640]{1,0:T(8,128)(2,1)S(1)} %get-tuple-element.71), channel_id=1, source_target_pairs={{0,32},{4,36},{8,40},{12,44},{16,48},{20,52},{24,56},{28,60},{32,6... | collective-permute-start | bytes 307208 | tf_op jit(solution)/shard_map/ppermute | solution.py:27
  164.6 15.4 %collective-permute-start.17 = (bf16[80,640]{1,0:T(8,128)(2,1)S(1)}, bf16[80,640]{1,0:T(8,128)(2,1)S(1)}, u32[]{:S(2)}, u32[]{:S(2)}) collective-permute-start(bf16[80,640]{1,0:T(8,128)(2,1)S(1)} %get-tuple-element.72), channel_id=1, source_target_pairs={{0,16},{4,20},{8,24},{12,28},{16,0},{20,4},{24,8},{28,12},{32,48},... | collective-permute-start | bytes 307208 | tf_op jit(solution)/shard_map/ppermute | solution.py:33
  165.6 14.4 %collective-permute-start.16 = (bf16[80,640]{1,0:T(8,128)(2,1)S(1)}, bf16[80,640]{1,0:T(8,128)(2,1)S(1)}, u32[]{:S(2)}, u32[]{:S(2)}) collective-permute-start(bf16[80,640]{1,0:T(8,128)(2,1)S(1)} %get-tuple-element.73), channel_id=1, source_target_pairs={{0,24},{4,28},{8,0},{12,4},{16,8},{20,12},{24,16},{28,20},{32,56},... | collective-permute-start | bytes 307208 | tf_op jit(solution)/shard_map/ppermute | solution.py:33
  176.4 20.0 %collective-permute-start.21 = (bf16[512,640]{1,0:T(8,128)(2,1)S(1)}, bf16[512,640]{1,0:T(8,128)(2,1)S(1)}, u32[]{:S(2)}, u32[]{:S(2)}) collective-permute-start(bf16[512,640]{1,0:T(8,128)(2,1)S(1)} %fusion.29), channel_id=1, source_target_pairs={{0,1},{1,2},{2,3},{3,0},{4,5},{5,6},{6,7},{7,4},{8,9},{9,10},{10,1... | collective-permute-start | bytes 1966088 | tf_op jit(solution)/shard_map/ppermute | solution.py:39
  176.4 38.8 %collective-permute-start.23 = (bf16[512,640]{1,0:T(8,128)(2,1)S(1)}, bf16[512,640]{1,0:T(8,128)(2,1)S(1)}, u32[]{:S(2)}, u32[]{:S(2)}) collective-permute-start(bf16[512,640]{1,0:T(8,128)(2,1)S(1)} %fusion.32), channel_id=1, source_target_pairs={{0,2},{1,3},{2,0},{3,1},{4,6},{5,7},{6,4},{7,5},{8,10},{9,11},{10,... | collective-permute-start | bytes 1966088 | tf_op jit(solution)/shard_map/ppermute | solution.py:39
  180.0 35.2 %collective-permute-start.22 = (bf16[512,640]{1,0:T(8,128)(2,1)S(1)}, bf16[512,640]{1,0:T(8,128)(2,1)S(1)}, u32[]{:S(2)}, u32[]{:S(2)}) collective-permute-start(bf16[512,640]{1,0:T(8,128)(2,1)S(1)} %fusion.35), channel_id=1, source_target_pairs={{0,3},{1,0},{2,1},{3,2},{4,7},{5,4},{6,5},{7,6},{8,11},{9,8},{10,9... | collective-permute-start | bytes 1966088 | tf_op jit(solution)/shard_map/ppermute | solution.py:39
  180.2 13.6 %collective-permute-start.24 = (bf16[160,640]{1,0:T(8,128)(2,1)S(1)}, bf16[160,640]{1,0:T(8,128)(2,1)S(1)}, u32[]{:S(2)}, u32[]{:S(2)}) collective-permute-start(bf16[160,640]{1,0:T(8,128)(2,1)S(1)} %fusion.44), channel_id=1, source_target_pairs={{0,0},{1,32},{2,64},{3,96},{4,4},{5,36},{6,68},{7,100},{8,8},{9,40... | collective-permute-start | bytes 614408 | tf_op jit(solution)/shard_map/ppermute | solution.py:52
  (16 other events, 111.8 us)
Sparse Core Ops, SparseCore 0:
  24.6 59.9 all-gather.1
where the time goes:
time: 226 us; the launch traced here: 224 us
  waiting for transfers between devices  84.5 us (37%)
  starting transfers between devices  48.4 us (21%)
  Pallas kernels  45.8 us (20%)
  matrix products  16 us (7%)
  between operations  14.3 us (6%)
  local copies, waits for them, and re-layouts  8.7 us (4%)
  other arithmetic  6.16 us (3%)
    ppermute x6, waiting for transfers between devices, along_y(): return lax.ppermute(value, 'mp', [(y, (y + shift) % NY) for y in range(NY)])  36.4 us
    all_to_all x1, waiting for transfers between devices, local(): lax.all_to_all(send_rows, 'dp', split_axis=0, concat_axis=0, tiled=True)  29 us
    pallas_call x2, Pallas kernels, attend(): pl.pallas_call(functools.partial(attend_kernel, first=first), out_shape=j...  19.7 us
    ppermute x2, starting transfers between devices, swap_xy(): return lax.ppermute(value, ('dp', 'mp'), pairs)  10.6 us
    ppermute x2, waiting for transfers between devices, swap_xy(): return lax.ppermute(value, ('dp', 'mp'), pairs)  9.62 us
    ppermute x6, starting transfers between devices, along_x(): lax.ppermute(value, 'dp', [(place(x, z, c), place(x + shift, z, c)) for x...  8.9 us
    pallas_call x1, Pallas kernels, grad_parts(): pl.pallas_call(grad_kernel, out_shape=(shape, shape), in_specs=[pl.BlockS...  8.79 us
    all_to_all x1, starting transfers between devices, local(): lax.all_to_all(send_rows, 'dp', split_axis=0, concat_axis=0, tiled=True)  8.47 us
  transfers between devices with their start and end apart: 27, of which 11 were waited for; matrix products, arithmetic and copies ran while one was open for 11% of the time, Pallas kernels for 20%

commit v1 on v0

--- a/solution.py
+++ b/solution.py
@@ -319,14 +319,14 @@
     half = row_count // 2
     caches = (fresh_keys, fresh_vals, key_cache, value_cache)
     first = attend(lengths, queries, *caches, 0, half)
-    lengths, first, weight_tile = lax.optimization_barrier((lengths, first, weight_tile))
     second = attend(lengths, queries, *caches, half, half)
-    weight = lax.all_gather(weight_tile, "dp", axis=0, tiled=True)
-    weight = weight.reshape(NX, -1, feat_width)
-
     send_rows = pack(goes_to, facts, first, second)
     got_rows = lax.all_to_all(send_rows, "dp", split_axis=0, concat_axis=0, tiled=True)
     acts, word = unpack(block[None], got_rows)
+
+    weight_tile, _ = lax.optimization_barrier((weight_tile, got_rows))
+    weight = lax.all_gather(weight_tile, "dp", axis=0, tiled=True)
+    weight = weight.reshape(NX, -1, feat_width)
 
     mine = [acts] + [along_y(acts, s) for s in (1, 2, 3)]
     theirs = [to_partner(block_cols) for block_cols in mine]
@@ -350,8 +350,8 @@
     grad_blocks = [
         jnp.dot(signal, columns(y + s), preferred_element_type=F32).astype(BF) for s in range(NY)
     ]
-    more_a, more_b, grad_blocks = lax.optimization_barrier((more_a, more_b, grad_blocks))
     more_grad = [along_y(grad_blocks[s], s) for s in (1, 3, 2)]
+    more_a, more_b, more_grad = lax.optimization_barrier((more_a, more_b, more_grad))
 
     part_a = total(part_a[0], *more_a).astype(BF)
     part_b = total(part_b[0], *more_b).astype(BF)

time: 226 us -> 210 us (0.929)
  waiting for transfers between devices: 84.5 us -> 74 us
  starting transfers between devices: 48.4 us -> 41.8 us
    all_to_all x1, waiting for transfers between devices: 29 us -> 0.01 us  [local(): lax.all_to_all(send_rows, 'dp', split_axis=0, concat_axis=0, tiled=True)]
    ppermute x2, waiting for transfers between devices: 9.62 us -> 32.3 us  [swap_xy(): return lax.ppermute(value, ('dp', 'mp'), pairs)]
    ppermute x5, starting transfers between devices: 6.91 us -> 0.61 us  [to_partner(): return lax.ppermute(value, 'dp', [(d, d ^ 1) for d in range(32)])]
    ppermute x6, waiting for transfers between devices: 36.4 us -> 30.3 us  [along_y(): return lax.ppermute(value, 'mp', [(y, (y + shift) % NY) for y in range(NY)])]
    ppermute x6, starting transfers between devices: 5.6 us -> 8.46 us  [along_y(): return lax.ppermute(value, 'mp', [(y, (y + shift) % NY) for y in range(NY)])]
    ppermute x2, starting transfers between devices: 10.6 us -> 8.1 us  [swap_xy(): return lax.ppermute(value, ('dp', 'mp'), pairs)]
  transfers between devices with their start and end apart: 27 -> 27, of which waited for: 11 -> 12; matrix products, arithmetic and copies ran while one was open for 11% -> 12% of each run, Pallas kernels for 20% -> 11%
where the time goes in v1:
time: 210 us; the launch traced here: 207 us
  waiting for transfers between devices  74 us (35%)
  Pallas kernels  46 us (22%)
  starting transfers between devices  41.8 us (20%)
  matrix products  15.9 us (8%)
  between operations  14.3 us (7%)
  local copies, waits for them, and re-layouts  8.98 us (4%)
  other arithmetic  6 us (3%)
    ppermute x2, waiting for transfers between devices, swap_xy(): return lax.ppermute(value, ('dp', 'mp'), pairs)  32.3 us
    ppermute x6, waiting for transfers between devices, along_y(): return lax.ppermute(value, 'mp', [(y, (y + shift) % NY) for y in range(NY)])  30.3 us
    pallas_call x2, Pallas kernels, attend(): pl.pallas_call(functools.partial(attend_kernel, first=first), out_shape=j...  19.7 us
    ppermute x6, starting transfers between devices, along_z(): lax.ppermute(value, 'dp', [(place(x, z, c), place(x, z + shift, c)) for x...  9.21 us
    pallas_call x1, Pallas kernels, grad_parts(): pl.pallas_call(grad_kernel, out_shape=(shape, shape), in_specs=[pl.BlockS...  9.07 us
    all_to_all x1, starting transfers between devices, local(): lax.all_to_all(send_rows, 'dp', split_axis=0, concat_axis=0, tiled=True)  8.58 us
    ppermute x6, starting transfers between devices, along_y(): return lax.ppermute(value, 'mp', [(y, (y + shift) % NY) for y in range(NY)])  8.46 us
    dot_general x4, matrix products, local(): lax.dot_general(mine[s], columns(y - s + NY), (((1,), (1,)), ((), ())), p...  8.11 us
  transfers between devices with their start and end apart: 27, of which 12 were waited for; matrix products, arithmetic and copies ran while one was open for 12% of the time, Pallas kernels for 11%

profile of v1, /device:TPU:4, one launch (start us, length us, event | category | flops | bytes accessed | tf_op | source)
XLA Modules:
  0.0 207.0 jit_solution(8970081360490999081)
XLA Ops:
  7.2 9.8 %attend.3.b_ref = bf16[256,640]{1,0:T(8,128)(2,1)} custom-call(s32[128]{0:T(128)} %lengths_ref.3, bf16[128,4,640]{2,1,0:T(4,128)(2,1)} %q_ref.3, bf16[512,128]{1,0:T(8,128)(2,1)} %bitcast.107, bf16[512,128]{1,0:T(8,128)(2,1)} %bitcast.109, bf16[128,256,128]{2,1,0:T(8,128)(2,1)} %k_ref.3, bf16[128,256,128]{2,1,0:T(8,128)(2,1)} %v_ref.3), custom_call_target="tpu_custom_call" | custom-call | tf_op jit(solution)/shard_map/attend/pallas_call | solution.py:116
  17.0 9.9 %attend.2.a_ref = bf16[256,640]{1,0:T(8,128)(2,1)} custom-call(s32[128]{0:T(128)} %lengths_ref.3, bf16[128,4,640]{2,1,0:T(4,128)(2,1)} %q_ref.3, bf16[512,128]{1,0:T(8,128)(2,1)} %bitcast.108, bf16[512,128]{1,0:T(8,128)(2,1)} %bitcast.110, bf16[128,256,128]{2,1,0:T(8,128)(2,1)} %k_ref.3, bf16[128,256,128]{2,1,0:T(8,128)(2,1)} %v_ref.3), custom_call_target="tpu_custom_call" | custom-call | tf_op jit(solution)/shard_map/attend/pallas_call | solution.py:116
  28.5 3.8 %pack.1 = bf16[32,40,640]{2,1,0:T(8,128)(2,1)} custom-call(s32[1,512]{1,0:T(1,128)} %add.177.goes_ref, bf16[8,640]{1,0:T(8,128)(2,1)} %convert_convert_fusion.facts_ref, bf16[256,640]{1,0:T(8,128)(2,1)} %attend.2.a_ref, bf16[256,640]{1,0:T(8,128)(2,1)} %attend.3.b_ref), custom_call_target="tpu_custom_call" | custom-call | tf_op jit(solution)/shard_map/pack/pallas_call | solution.py:153
  32.3 8.6 %all-to-all-start = ((bf16[32,40,640]{2,1,0:T(8,128)(2,1)}), bf16[32,40,640]{2,1,0:T(8,128)(2,1)S(1)}, u32[]{:S(2)}, u32[]{:S(2)}) async-start(bf16[32,40,640]{2,1,0:T(8,128)(2,1)} %pack.1), calls=%async_computation | async-start | bytes 3276800 | tf_op jit(solution)/shard_map/all_to_all | solution.py:324
  41.0 4.8 %collective-permute-start.14 = (bf16[160,640]{1,0:T(8,128)(2,1)S(1)}, bf16[160,640]{1,0:T(8,128)(2,1)S(1)}, u32[]{:S(2)}, u32[]{:S(2)}) collective-permute-start(bf16[160,640]{1,0:T(8,128)(2,1)S(1)} %copy-done.11), channel_id=1, source_target_pairs={{0,0},{1,32},{2,64},{3,96},{4,4},{5,36},{6,68},{7,100},{8,8},{9,40... | collective-permute-start | bytes 614408 | tf_op jit(solution)/shard_map/ppermute | solution.py:52
  45.7 24.5 %collective-permute-done.14 = bf16[160,640]{1,0:T(8,128)(2,1)S(1)} collective-permute-done((bf16[160,640]{1,0:T(8,128)(2,1)S(1)}, bf16[160,640]{1,0:T(8,128)(2,1)S(1)}, u32[]{:S(2)}, u32[]{:S(2)}) %collective-permute-start.14) | collective-permute-done | bytes 204832 | tf_op jit(solution)/shard_map/ppermute | solution.py:52
  71.6 5.6 %unpack.1 = (bf16[512,640]{1,0:T(8,128)(2,1)}, s32[512,1]{1,0:T(8,128)}) custom-call(s32[1]{0:T(128)} %bitcast.11.block_ref, bf16[32,40,640]{2,1,0:T(8,128)(2,1)} %copy-done, bf16[1280,640]{1,0:T(8,128)(2,1)} %bitcast.103), custom_call_target="tpu_custom_call" | custom-call | tf_op jit(solution)/shard_map/unpack/pallas_call | solution.py:187
  80.5 7.8 %weigh.1 = bf16[512,1280]{1,0:T(8,128)(2,1)} custom-call(bf16[32,40,640]{2,1,0:T(8,128)(2,1)} %copy-done, s32[512,1]{1,0:T(8,128)} %get-tuple-element.29.word_ref, bf16[512,1280]{1,0:T(8,128)(2,1)} %cot_ref.1), custom_call_target="tpu_custom_call" | custom-call | tf_op jit(solution)/shard_map/weigh/pallas_call | solution.py:229
  91.1 15.8 %collective-permute-done.3.refs_3_ = bf16[512,640]{1,0:T(8,128)(2,1)S(1)} collective-permute-done((bf16[512,640]{1,0:T(8,128)(2,1)}, bf16[512,640]{1,0:T(8,128)(2,1)S(1)}, u32[]{:S(2)}, u32[]{:S(2)}) %collective-permute-start.3) | collective-permute-done | bytes 655392 | tf_op jit(solution)/shard_map/ppermute | solution.py:39
  107.4 3.2 %collective-permute-done.1.refs_1_ = bf16[512,640]{1,0:T(8,128)(2,1)} collective-permute-done((bf16[512,640]{1,0:T(8,128)(2,1)}, bf16[512,640]{1,0:T(8,128)(2,1)}, u32[]{:S(2)}, u32[]{:S(2)}) %collective-permute-start.1) | collective-permute-done | bytes 655392 | tf_op jit(solution)/shard_map/ppermute | solution.py:39
  113.0 9.1 %grad_parts.1 = (bf16[4,4,80,640]{3,2,1,0:T(8,128)(2,1)}, bf16[4,4,80,640]{3,2,1,0:T(8,128)(2,1)}) custom-call(s32[3]{0:T(128)} %pad_add_fusion.where_ref, bf16[640,1024]{1,0:T(8,128)(2,1)} %pad_maximum_fusion.left_ref, bf16[512,640]{1,0:T(8,128)(2,1)} %get-tuple-element.41.refs_0_, bf16[512,640]{1,0:T(8,128)(2,1)} %collective-permute-done.1.refs_1_, ...), custom_call_target="tpu_custom_call" | custom-call | tf_op jit(solution)/shard_map/grad_parts/pallas_call | solution.py:265
  122.1 2.5 %slice_bitcast_fusion = (bf16[4,80,640]{2,1,0:T(8,128)(2,1)}, bf16[4,80,640]{2,1,0:T(8,128)(2,1)}, bf16[4,80,640]{2,1,0:T(8,128)(2,1)}) fusion(bf16[4,4,80,640]{3,2,1,0:T(8,128)(2,1)} %get-tuple-element.32), kind=kLoop, calls=%fused_computation.45 | loop fusion | bytes 2457600 | tf_op jit(solution)/shard_map/squeeze | solution.py:344
  124.5 3.0 %collective-permute-start.13 = (bf16[4,80,640]{2,1,0:T(8,128)(2,1)}, bf16[4,80,640]{2,1,0:T(8,128)(2,1)}, u32[]{:S(2)}, u32[]{:S(2)}) collective-permute-start(bf16[4,80,640]{2,1,0:T(8,128)(2,1)} %get-tuple-element.55), channel_id=1, source_target_pairs={{0,16},{4,20},{8,24},{12,28},{16,0},{20,4},{24,8},{28,12},{32,48},... | collective-permute-start | bytes 1228808 | tf_op jit(solution)/shard_map/ppermute | solution.py:33
  132.8 2.8 %fusion.35 = bf16[512,640]{1,0:T(8,128)(2,1)S(1)} fusion(bf16[512,1280]{1,0:T(8,128)(2,1)S(1)} %copy-done.1, bf16[4,1280,640]{2,1,0:T(8,128)(2,1)} %bitcast.111, s32[]{:T(128)S(6)} %select_n.105), kind=kOutput, calls=%fused_computation.30 | convolution fusion | flops 839188480 | bytes 3604484 | tf_op jit(solution)/shard_map/dot_general | solution.py:351
  135.6 2.6 %fusion.32 = bf16[512,640]{1,0:T(8,128)(2,1)S(1)} fusion(bf16[512,1280]{1,0:T(8,128)(2,1)S(1)} %copy-done.1, bf16[4,1280,640]{2,1,0:T(8,128)(2,1)} %bitcast.112, s32[]{:T(128)S(6)} %select_n.103), kind=kOutput, calls=%fused_computation.29 | convolution fusion | flops 839188480 | bytes 3604484 | tf_op jit(solution)/shard_map/dot_general | solution.py:351
  140.7 3.2 %collective-permute-start.16 = (bf16[512,640]{1,0:T(8,128)(2,1)S(1)}, bf16[512,640]{1,0:T(8,128)(2,1)S(1)}, u32[]{:S(2)}, u32[]{:S(2)}) collective-permute-start(bf16[512,640]{1,0:T(8,128)(2,1)S(1)} %fusion.29), channel_id=1, source_target_pairs={{0,3},{1,0},{2,1},{3,2},{4,7},{5,4},{6,5},{7,6},{8,11},{9,8},{10,9... | collective-permute-start | bytes 1966088 | tf_op jit(solution)/shard_map/ppermute | solution.py:39
  144.0 2.7 %collective-permute-done.12 = bf16[4,80,640]{2,1,0:T(8,128)(2,1)} collective-permute-done((bf16[4,80,640]{2,1,0:T(8,128)(2,1)}, bf16[4,80,640]{2,1,0:T(8,128)(2,1)}, u32[]{:S(2)}, u32[]{:S(2)}) %collective-permute-start.12) | collective-permute-done | bytes 409632 | tf_op jit(solution)/shard_map/ppermute | solution.py:33
  153.0 2.3 %fusion.6 = f32[512,1280]{1,0:T(8,128)S(1)} fusion(bf16[512,640]{1,0:T(8,128)(2,1)} %collective-permute-done.2.refs_2_, bf16[4,1280,640]{2,1,0:T(8,128)(2,1)S(1)} %bitcast.116, s32[]{:T(128)S(6)} %select_n.103), kind=kOutput, calls=%fused_computation.7 | convolution fusion | flops 838860800 | bytes 4915204 | tf_op jit(solution)/shard_map/dot_general | solution.py:364
  156.5 4.8 %collective-permute-done.9 = bf16[4,80,640]{2,1,0:T(8,128)(2,1)S(1)} collective-permute-done((bf16[4,80,640]{2,1,0:T(8,128)(2,1)S(1)}, bf16[4,80,640]{2,1,0:T(8,128)(2,1)S(1)}, u32[]{:S(2)}, u32[]{:S(2)}) %collective-permute-start.9) | collective-permute-done | bytes 409632 | tf_op jit(solution)/shard_map/ppermute | solution.py:27
  161.4 9.6 %collective-permute-done.16 = bf16[512,640]{1,0:T(8,128)(2,1)S(1)} collective-permute-done((bf16[512,640]{1,0:T(8,128)(2,1)S(1)}, bf16[512,640]{1,0:T(8,128)(2,1)S(1)}, u32[]{:S(2)}, u32[]{:S(2)}) %collective-permute-start.16) | collective-permute-done | bytes 655392 | tf_op jit(solution)/shard_map/ppermute | solution.py:39
  178.8 2.3 %collective-permute-start.19 = (bf16[80,640]{1,0:T(8,128)(2,1)S(1)}, bf16[80,640]{1,0:T(8,128)(2,1)S(1)}, u32[]{:S(2)}, u32[]{:S(2)}) collective-permute-start(bf16[80,640]{1,0:T(8,128)(2,1)S(1)} %get-tuple-element.67), channel_id=1, source_target_pairs={{0,24},{4,28},{8,0},{12,4},{16,8},{20,12},{24,16},{28,20},{32,56},... | collective-permute-start | bytes 307208 | tf_op jit(solution)/shard_map/ppermute | solution.py:33
  184.5 2.5 %collective-permute-done.18 = bf16[80,640]{1,0:T(8,128)(2,1)S(1)} collective-permute-done((bf16[80,640]{1,0:T(8,128)(2,1)S(1)}, bf16[80,640]{1,0:T(8,128)(2,1)S(1)}, u32[]{:S(2)}, u32[]{:S(2)}) %collective-permute-start.18) | collective-permute-done | bytes 102432 | tf_op jit(solution)/shard_map/ppermute | solution.py:33
  187.2 3.3 %collective-permute-start.24 = (bf16[160,640]{1,0:T(8,128)(2,1)S(1)}, bf16[160,640]{1,0:T(8,128)(2,1)S(1)}, u32[]{:S(2)}, u32[]{:S(2)}) collective-permute-start(bf16[160,640]{1,0:T(8,128)(2,1)S(1)} %fusion.44), channel_id=1, source_target_pairs={{0,0},{1,32},{2,64},{3,96},{4,4},{5,36},{6,68},{7,100},{8,8},{9,40... | collective-permute-start | bytes 614408 | tf_op jit(solution)/shard_map/ppermute | solution.py:52
  191.7 7.8 %collective-permute-done.24 = bf16[160,640]{1,0:T(8,128)(2,1)S(1)} collective-permute-done((bf16[160,640]{1,0:T(8,128)(2,1)S(1)}, bf16[160,640]{1,0:T(8,128)(2,1)S(1)}, u32[]{:S(2)}, u32[]{:S(2)}) %collective-permute-start.24) | collective-permute-done | bytes 204832 | tf_op jit(solution)/shard_map/ppermute | solution.py:52
  (96 shorter events, 40.5 us)
Async XLA Ops:
  32.3 37.9 %all-to-all-start = ((bf16[32,40,640]{2,1,0:T(8,128)(2,1)}), bf16[32,40,640]{2,1,0:T(8,128)(2,1)S(1)}, u32[]{:S(2)}, u32[]{:S(2)}) async-start(bf16[32,40,640]{2,1,0:T(8,128)(2,1)} %pack.1), calls=%async_computation | async-start | bytes 3276800 | tf_op jit(solution)/shard_map/all_to_all | solution.py:324
  40.9 92.0 %all-gather.2.cloned.1.call-start = ((), (), s32[]{:S(2)}) async-start(), calls=%async_computation.1 | async-start | bytes 6758400 | tf_op jit(solution)/shard_map/all_gather | solution.py:328
  41.0 29.3 %collective-permute-start.14 = (bf16[160,640]{1,0:T(8,128)(2,1)S(1)}, bf16[160,640]{1,0:T(8,128)(2,1)S(1)}, u32[]{:S(2)}, u32[]{:S(2)}) collective-permute-start(bf16[160,640]{1,0:T(8,128)(2,1)S(1)} %copy-done.11), channel_id=1, source_target_pairs={{0,0},{1,32},{2,64},{3,96},{4,4},{5,36},{6,68},{7,100},{8,8},{9,40... | collective-permute-start | bytes 614408 | tf_op jit(solution)/shard_map/ppermute | solution.py:52
  77.2 29.7 %collective-permute-start.3 = (bf16[512,640]{1,0:T(8,128)(2,1)}, bf16[512,640]{1,0:T(8,128)(2,1)S(1)}, u32[]{:S(2)}, u32[]{:S(2)}) collective-permute-start(bf16[512,640]{1,0:T(8,128)(2,1)} %get-tuple-element.41.refs_0_), channel_id=1, source_target_pairs={{0,3},{1,0},{2,1},{3,2},{4,7},{5,4},{6,5},{7,6},{8,11},{9,8},{10,9... | collective-permute-start | bytes 1966088 | tf_op jit(solution)/shard_map/ppermute | solution.py:39
  79.0 27.9 %collective-permute-start.2 = (bf16[512,640]{1,0:T(8,128)(2,1)}, bf16[512,640]{1,0:T(8,128)(2,1)}, u32[]{:S(2)}, u32[]{:S(2)}) collective-permute-start(bf16[512,640]{1,0:T(8,128)(2,1)} %get-tuple-element.41.refs_0_), channel_id=1, source_target_pairs={{0,2},{1,3},{2,0},{3,1},{4,6},{5,7},{6,4},{7,5},{8,10},{9,11},{10,... | collective-permute-start | bytes 1966088 | tf_op jit(solution)/shard_map/ppermute | solution.py:39
  80.5 30.1 %collective-permute-start.1 = (bf16[512,640]{1,0:T(8,128)(2,1)}, bf16[512,640]{1,0:T(8,128)(2,1)}, u32[]{:S(2)}, u32[]{:S(2)}) collective-permute-start(bf16[512,640]{1,0:T(8,128)(2,1)} %get-tuple-element.41.refs_0_), channel_id=1, source_target_pairs={{0,1},{1,2},{2,3},{3,0},{4,5},{5,6},{6,7},{7,4},{8,9},{9,10},{10,1... | collective-permute-start | bytes 1966088 | tf_op jit(solution)/shard_map/ppermute | solution.py:39
  90.1 21.1 %collective-permute-start = (bf16[640,512]{1,0:T(8,128)(2,1)S(1)}, bf16[640,512]{1,0:T(8,128)(2,1)S(1)}, u32[]{:S(2)}, u32[]{:S(2)}) collective-permute-start(bf16[640,512]{1,0:T(8,128)(2,1)S(1)} %get-tuple-element.62), channel_id=1, source_target_pairs={{0,4},{4,0},{8,12},{12,8},{16,20},{20,16},{24,28},{28,24},{32,36},... | collective-permute-start | bytes 1966088 | tf_op jit(solution)/shard_map/ppermute | solution.py:43
  91.1 21.4 %collective-permute-start.4 = (bf16[512,640]{1,0:T(8,128)(2,1)S(1)}, bf16[512,640]{1,0:T(8,128)(2,1)}, u32[]{:S(2)}, u32[]{:S(2)}) collective-permute-start(bf16[512,640]{1,0:T(8,128)(2,1)S(1)} %copy-done.2), channel_id=1, source_target_pairs={{0,4},{4,0},{8,12},{12,8},{16,20},{20,16},{24,28},{28,24},{32,36},... | collective-permute-start | bytes 1966088 | tf_op jit(solution)/shard_map/ppermute | solution.py:43
  124.5 16.2 %collective-permute-start.13 = (bf16[4,80,640]{2,1,0:T(8,128)(2,1)}, bf16[4,80,640]{2,1,0:T(8,128)(2,1)}, u32[]{:S(2)}, u32[]{:S(2)}) collective-permute-start(bf16[4,80,640]{2,1,0:T(8,128)(2,1)} %get-tuple-element.55), channel_id=1, source_target_pairs={{0,16},{4,20},{8,24},{12,28},{16,0},{20,4},{24,8},{28,12},{32,48},... | collective-permute-start | bytes 1228808 | tf_op jit(solution)/shard_map/ppermute | solution.py:33
  127.5 19.2 %collective-permute-start.12 = (bf16[4,80,640]{2,1,0:T(8,128)(2,1)}, bf16[4,80,640]{2,1,0:T(8,128)(2,1)}, u32[]{:S(2)}, u32[]{:S(2)}) collective-permute-start(bf16[4,80,640]{2,1,0:T(8,128)(2,1)} %get-tuple-element.56), channel_id=1, source_target_pairs={{0,24},{4,28},{8,0},{12,4},{16,8},{20,12},{24,16},{28,20},{32,56},... | collective-permute-start | bytes 1228808 | tf_op jit(solution)/shard_map/ppermute | solution.py:33
  128.9 22.0 %collective-permute-start.11 = (bf16[4,80,640]{2,1,0:T(8,128)(2,1)}, bf16[4,80,640]{2,1,0:T(8,128)(2,1)}, u32[]{:S(2)}, u32[]{:S(2)}) collective-permute-start(bf16[4,80,640]{2,1,0:T(8,128)(2,1)} %get-tuple-element.57), channel_id=1, source_target_pairs={{0,8},{4,12},{8,16},{12,20},{16,24},{20,28},{24,0},{28,4},{32,40},... | collective-permute-start | bytes 1228808 | tf_op jit(solution)/shard_map/ppermute | solution.py:33
  130.6 20.6 %collective-permute-start.10 = (bf16[4,80,640]{2,1,0:T(8,128)(2,1)}, bf16[4,80,640]{2,1,0:T(8,128)(2,1)}, u32[]{:S(2)}, u32[]{:S(2)}) collective-permute-start(bf16[4,80,640]{2,1,0:T(8,128)(2,1)} %get-tuple-element.58), channel_id=1, source_target_pairs={{0,64},{4,68},{8,72},{12,76},{16,80},{20,84},{24,88},{28,92},{32,9... | collective-permute-start | bytes 1228808 | tf_op jit(solution)/shard_map/ppermute | solution.py:27
  140.7 20.8 %collective-permute-start.15 = (bf16[512,640]{1,0:T(8,128)(2,1)S(1)}, bf16[512,640]{1,0:T(8,128)(2,1)S(1)}, u32[]{:S(2)}, u32[]{:S(2)}) collective-permute-start(bf16[512,640]{1,0:T(8,128)(2,1)S(1)} %fusion.26), channel_id=1, source_target_pairs={{0,1},{1,2},{2,3},{3,0},{4,5},{5,6},{6,7},{7,4},{8,9},{9,10},{10,1... | collective-permute-start | bytes 1966088 | tf_op jit(solution)/shard_map/ppermute | solution.py:39
  140.7 30.2 %collective-permute-start.16 = (bf16[512,640]{1,0:T(8,128)(2,1)S(1)}, bf16[512,640]{1,0:T(8,128)(2,1)S(1)}, u32[]{:S(2)}, u32[]{:S(2)}) collective-permute-start(bf16[512,640]{1,0:T(8,128)(2,1)S(1)} %fusion.29), channel_id=1, source_target_pairs={{0,3},{1,0},{2,1},{3,2},{4,7},{5,4},{6,5},{7,6},{8,11},{9,8},{10,9... | collective-permute-start | bytes 1966088 | tf_op jit(solution)/shard_map/ppermute | solution.py:39
  146.7 26.1 %collective-permute-start.17 = (bf16[512,640]{1,0:T(8,128)(2,1)S(1)}, bf16[512,640]{1,0:T(8,128)(2,1)S(1)}, u32[]{:S(2)}, u32[]{:S(2)}) collective-permute-start(bf16[512,640]{1,0:T(8,128)(2,1)S(1)} %fusion.32), channel_id=1, source_target_pairs={{0,2},{1,3},{2,0},{3,1},{4,6},{5,7},{6,4},{7,5},{8,10},{9,11},{10,... | collective-permute-start | bytes 1966088 | tf_op jit(solution)/shard_map/ppermute | solution.py:39
  150.9 10.5 %collective-permute-start.9 = (bf16[4,80,640]{2,1,0:T(8,128)(2,1)S(1)}, bf16[4,80,640]{2,1,0:T(8,128)(2,1)S(1)}, u32[]{:S(2)}, u32[]{:S(2)}) collective-permute-start(bf16[4,80,640]{2,1,0:T(8,128)(2,1)S(1)} %copy-done.7), channel_id=1, source_target_pairs={{0,96},{4,100},{8,104},{12,108},{16,112},{20,116},{24,120},{28,124... | collective-permute-start | bytes 1228808 | tf_op jit(solution)/shard_map/ppermute | solution.py:27
  151.1 10.3 %collective-permute-start.8 = (bf16[4,80,640]{2,1,0:T(8,128)(2,1)S(1)}, bf16[4,80,640]{2,1,0:T(8,128)(2,1)S(1)}, u32[]{:S(2)}, u32[]{:S(2)}) collective-permute-start(bf16[4,80,640]{2,1,0:T(8,128)(2,1)S(1)} %get-tuple-element.60), channel_id=1, source_target_pairs={{0,32},{4,36},{8,40},{12,44},{16,48},{20,52},{24,56},{28,60},{32,6... | collective-permute-start | bytes 1228808 | tf_op jit(solution)/shard_map/ppermute | solution.py:27
  174.8 6.4 %collective-permute-start.23 = (bf16[80,640]{1,0:T(8,128)(2,1)S(1)}, bf16[80,640]{1,0:T(8,128)(2,1)S(1)}, u32[]{:S(2)}, u32[]{:S(2)}) collective-permute-start(bf16[80,640]{1,0:T(8,128)(2,1)S(1)} %get-tuple-element.63), channel_id=1, source_target_pairs={{0,64},{4,68},{8,72},{12,76},{16,80},{20,84},{24,88},{28,92},{32,9... | collective-permute-start | bytes 307208 | tf_op jit(solution)/shard_map/ppermute | solution.py:27
  175.2 8.6 %collective-permute-start.22 = (bf16[80,640]{1,0:T(8,128)(2,1)S(1)}, bf16[80,640]{1,0:T(8,128)(2,1)S(1)}, u32[]{:S(2)}, u32[]{:S(2)}) collective-permute-start(bf16[80,640]{1,0:T(8,128)(2,1)S(1)} %get-tuple-element.64), channel_id=1, source_target_pairs={{0,96},{4,100},{8,104},{12,108},{16,112},{20,116},{24,120},{28,124... | collective-permute-start | bytes 307208 | tf_op jit(solution)/shard_map/ppermute | solution.py:27
  177.0 6.8 %collective-permute-start.21 = (bf16[80,640]{1,0:T(8,128)(2,1)S(1)}, bf16[80,640]{1,0:T(8,128)(2,1)S(1)}, u32[]{:S(2)}, u32[]{:S(2)}) collective-permute-start(bf16[80,640]{1,0:T(8,128)(2,1)S(1)} %get-tuple-element.65), channel_id=1, source_target_pairs={{0,32},{4,36},{8,40},{12,44},{16,48},{20,52},{24,56},{28,60},{32,6... | collective-permute-start | bytes 307208 | tf_op jit(solution)/shard_map/ppermute | solution.py:27
  177.2 7.3 %collective-permute-start.20 = (bf16[80,640]{1,0:T(8,128)(2,1)S(1)}, bf16[80,640]{1,0:T(8,128)(2,1)S(1)}, u32[]{:S(2)}, u32[]{:S(2)}) collective-permute-start(bf16[80,640]{1,0:T(8,128)(2,1)S(1)} %get-tuple-element.66), channel_id=1, source_target_pairs={{0,16},{4,20},{8,24},{12,28},{16,0},{20,4},{24,8},{28,12},{32,48},... | collective-permute-start | bytes 307208 | tf_op jit(solution)/shard_map/ppermute | solution.py:33
  178.8 5.7 %collective-permute-start.19 = (bf16[80,640]{1,0:T(8,128)(2,1)S(1)}, bf16[80,640]{1,0:T(8,128)(2,1)S(1)}, u32[]{:S(2)}, u32[]{:S(2)}) collective-permute-start(bf16[80,640]{1,0:T(8,128)(2,1)S(1)} %get-tuple-element.67), channel_id=1, source_target_pairs={{0,24},{4,28},{8,0},{12,4},{16,8},{20,12},{24,16},{28,20},{32,56},... | collective-permute-start | bytes 307208 | tf_op jit(solution)/shard_map/ppermute | solution.py:33
  181.2 5.9 %collective-permute-start.18 = (bf16[80,640]{1,0:T(8,128)(2,1)S(1)}, bf16[80,640]{1,0:T(8,128)(2,1)S(1)}, u32[]{:S(2)}, u32[]{:S(2)}) collective-permute-start(bf16[80,640]{1,0:T(8,128)(2,1)S(1)} %get-tuple-element.68), channel_id=1, source_target_pairs={{0,8},{4,12},{8,16},{12,20},{16,24},{20,28},{24,0},{28,4},{32,40},... | collective-permute-start | bytes 307208 | tf_op jit(solution)/shard_map/ppermute | solution.py:33
  187.2 12.3 %collective-permute-start.24 = (bf16[160,640]{1,0:T(8,128)(2,1)S(1)}, bf16[160,640]{1,0:T(8,128)(2,1)S(1)}, u32[]{:S(2)}, u32[]{:S(2)}) collective-permute-start(bf16[160,640]{1,0:T(8,128)(2,1)S(1)} %fusion.44), channel_id=1, source_target_pairs={{0,0},{1,32},{2,64},{3,96},{4,4},{5,36},{6,68},{7,100},{8,8},{9,40... | collective-permute-start | bytes 614408 | tf_op jit(solution)/shard_map/ppermute | solution.py:52
  (17 other events, 103.8 us)
Sparse Core Ops, SparseCore 0:
  71.1 49.3 all-gather.1

commit v2 on v1

--- a/solution.py
+++ b/solution.py
@@ -350,8 +350,9 @@
     grad_blocks = [
         jnp.dot(signal, columns(y + s), preferred_element_type=F32).astype(BF) for s in range(NY)
     ]
-    more_grad = [along_y(grad_blocks[s], s) for s in (1, 3, 2)]
-    more_a, more_b, more_grad = lax.optimization_barrier((more_a, more_b, more_grad))
+    far_grad = along_y(grad_blocks[2], 2)
+    near_grad = [along_y(grad_blocks[s], s) for s in (1, 3)]
+    more_a, more_b, far_grad = lax.optimization_barrier((more_a, more_b, far_grad))
 
     part_a = total(part_a[0], *more_a).astype(BF)
     part_b = total(part_b[0], *more_b).astype(BF)
@@ -373,7 +374,7 @@
     sum_b = total(part_b[0], *more_b)
     piece = (jnp.concatenate([sum_a, sum_b], axis=0) / 32).astype(BF)
     grad_proj = swap_xy(piece)
-    grad_attn = total(grad_blocks[0], *more_grad).astype(BF)
+    grad_attn = total(grad_blocks[0], *near_grad, far_grad).astype(BF)
     return (out_y, grad_attn, grad_proj)
 
 

time: 210 us -> 200 us (0.952); the launches traced: 207 us -> 199 us
  waiting for transfers between devices: 74 us -> 65.7 us
    ppermute x6, waiting for transfers between devices: 30.3 us -> 21.6 us  [along_y(): return lax.ppermute(value, 'mp', [(y, (y + shift) % NY) for y in range(NY)])]
  transfers between devices with their start and end apart: 27 -> 27, of which waited for: 12 -> 12; matrix products, arithmetic and copies ran while one was open for 12% -> 13% of each run, Pallas kernels for 11% -> 11%
where the time goes in v2:
time: 200 us; the launch traced here: 199 us
  waiting for transfers between devices  65.7 us (33%)
  Pallas kernels  46 us (23%)
  starting transfers between devices  42.5 us (21%)
  matrix products  15.9 us (8%)
  between operations  14.3 us (7%)
  local copies, waits for them, and re-layouts  8.98 us (4%)
  other arithmetic  6.01 us (3%)
    ppermute x2, waiting for transfers between devices, swap_xy(): return lax.ppermute(value, ('dp', 'mp'), pairs)  32.6 us
    ppermute x6, waiting for transfers between devices, along_y(): return lax.ppermute(value, 'mp', [(y, (y + shift) % NY) for y in range(NY)])  21.6 us
    pallas_call x2, Pallas kernels, attend(): pl.pallas_call(functools.partial(attend_kernel, first=first), out_shape=j...  19.7 us
    ppermute x2, starting transfers between devices, swap_xy(): return lax.ppermute(value, ('dp', 'mp'), pairs)  9.98 us
    pallas_call x1, Pallas kernels, grad_parts(): pl.pallas_call(grad_kernel, out_shape=(shape, shape), in_specs=[pl.BlockS...  9.07 us
    all_to_all x1, starting transfers between devices, local(): lax.all_to_all(send_rows, 'dp', split_axis=0, concat_axis=0, tiled=True)  8.58 us
    dot_general x4, matrix products, local(): lax.dot_general(mine[s], columns(y - s + NY), (((1,), (1,)), ((), ())), p...  8.13 us
    ppermute x6, starting transfers between devices, along_z(): lax.ppermute(value, 'dp', [(place(x, z, c), place(x, z + shift, c)) for x...  8.11 us
  transfers between devices with their start and end apart: 27, of which 12 were waited for; matrix products, arithmetic and copies ran while one was open for 13% of the time, Pallas kernels for 11%

profile of v2, /device:TPU:4, one launch (start us, length us, event | category | flops | bytes accessed | tf_op | source)
XLA Modules:
  0.0 199.4 jit_solution(11911727424244457687)
XLA Ops:
  7.2 9.8 %attend.3.b_ref = bf16[256,640]{1,0:T(8,128)(2,1)} custom-call(s32[128]{0:T(128)} %lengths_ref.3, bf16[128,4,640]{2,1,0:T(4,128)(2,1)} %q_ref.3, bf16[512,128]{1,0:T(8,128)(2,1)} %bitcast.107, bf16[512,128]{1,0:T(8,128)(2,1)} %bitcast.109, bf16[128,256,128]{2,1,0:T(8,128)(2,1)} %k_ref.3, bf16[128,256,128]{2,1,0:T(8,128)(2,1)} %v_ref.3), custom_call_target="tpu_custom_call" | custom-call | tf_op jit(solution)/shard_map/attend/pallas_call | solution.py:116
  17.0 9.9 %attend.2.a_ref = bf16[256,640]{1,0:T(8,128)(2,1)} custom-call(s32[128]{0:T(128)} %lengths_ref.3, bf16[128,4,640]{2,1,0:T(4,128)(2,1)} %q_ref.3, bf16[512,128]{1,0:T(8,128)(2,1)} %bitcast.108, bf16[512,128]{1,0:T(8,128)(2,1)} %bitcast.110, bf16[128,256,128]{2,1,0:T(8,128)(2,1)} %k_ref.3, bf16[128,256,128]{2,1,0:T(8,128)(2,1)} %v_ref.3), custom_call_target="tpu_custom_call" | custom-call | tf_op jit(solution)/shard_map/attend/pallas_call | solution.py:116
  28.5 3.8 %pack.1 = bf16[32,40,640]{2,1,0:T(8,128)(2,1)} custom-call(s32[1,512]{1,0:T(1,128)} %add.177.goes_ref, bf16[8,640]{1,0:T(8,128)(2,1)} %convert_convert_fusion.facts_ref, bf16[256,640]{1,0:T(8,128)(2,1)} %attend.2.a_ref, bf16[256,640]{1,0:T(8,128)(2,1)} %attend.3.b_ref), custom_call_target="tpu_custom_call" | custom-call | tf_op jit(solution)/shard_map/pack/pallas_call | solution.py:153
  32.3 8.6 %all-to-all-start = ((bf16[32,40,640]{2,1,0:T(8,128)(2,1)}), bf16[32,40,640]{2,1,0:T(8,128)(2,1)S(1)}, u32[]{:S(2)}, u32[]{:S(2)}) async-start(bf16[32,40,640]{2,1,0:T(8,128)(2,1)} %pack.1), calls=%async_computation | async-start | bytes 3276800 | tf_op jit(solution)/shard_map/all_to_all | solution.py:324
  41.0 4.8 %collective-permute-start.14 = (bf16[160,640]{1,0:T(8,128)(2,1)S(1)}, bf16[160,640]{1,0:T(8,128)(2,1)S(1)}, u32[]{:S(2)}, u32[]{:S(2)}) collective-permute-start(bf16[160,640]{1,0:T(8,128)(2,1)S(1)} %copy-done.11), channel_id=1, source_target_pairs={{0,0},{1,32},{2,64},{3,96},{4,4},{5,36},{6,68},{7,100},{8,8},{9,40... | collective-permute-start | bytes 614408 | tf_op jit(solution)/shard_map/ppermute | solution.py:52
  45.7 24.5 %collective-permute-done.14 = bf16[160,640]{1,0:T(8,128)(2,1)S(1)} collective-permute-done((bf16[160,640]{1,0:T(8,128)(2,1)S(1)}, bf16[160,640]{1,0:T(8,128)(2,1)S(1)}, u32[]{:S(2)}, u32[]{:S(2)}) %collective-permute-start.14) | collective-permute-done | bytes 204832 | tf_op jit(solution)/shard_map/ppermute | solution.py:52
  71.6 5.6 %unpack.1 = (bf16[512,640]{1,0:T(8,128)(2,1)}, s32[512,1]{1,0:T(8,128)}) custom-call(s32[1]{0:T(128)} %bitcast.11.block_ref, bf16[32,40,640]{2,1,0:T(8,128)(2,1)} %copy-done, bf16[1280,640]{1,0:T(8,128)(2,1)} %bitcast.103), custom_call_target="tpu_custom_call" | custom-call | tf_op jit(solution)/shard_map/unpack/pallas_call | solution.py:187
  80.5 7.8 %weigh.1 = bf16[512,1280]{1,0:T(8,128)(2,1)} custom-call(bf16[32,40,640]{2,1,0:T(8,128)(2,1)} %copy-done, s32[512,1]{1,0:T(8,128)} %get-tuple-element.27.word_ref, bf16[512,1280]{1,0:T(8,128)(2,1)} %cot_ref.1), custom_call_target="tpu_custom_call" | custom-call | tf_op jit(solution)/shard_map/weigh/pallas_call | solution.py:229
  91.1 15.8 %collective-permute-done.3.refs_3_ = bf16[512,640]{1,0:T(8,128)(2,1)S(1)} collective-permute-done((bf16[512,640]{1,0:T(8,128)(2,1)}, bf16[512,640]{1,0:T(8,128)(2,1)S(1)}, u32[]{:S(2)}, u32[]{:S(2)}) %collective-permute-start.3) | collective-permute-done | bytes 655392 | tf_op jit(solution)/shard_map/ppermute | solution.py:39
  107.4 3.2 %collective-permute-done.1.refs_1_ = bf16[512,640]{1,0:T(8,128)(2,1)} collective-permute-done((bf16[512,640]{1,0:T(8,128)(2,1)}, bf16[512,640]{1,0:T(8,128)(2,1)}, u32[]{:S(2)}, u32[]{:S(2)}) %collective-permute-start.1) | collective-permute-done | bytes 655392 | tf_op jit(solution)/shard_map/ppermute | solution.py:39
  113.0 9.1 %grad_parts.1 = (bf16[4,4,80,640]{3,2,1,0:T(8,128)(2,1)}, bf16[4,4,80,640]{3,2,1,0:T(8,128)(2,1)}) custom-call(s32[3]{0:T(128)} %pad_add_fusion.where_ref, bf16[640,1024]{1,0:T(8,128)(2,1)} %pad_maximum_fusion.left_ref, bf16[512,640]{1,0:T(8,128)(2,1)} %get-tuple-element.39.refs_0_, bf16[512,640]{1,0:T(8,128)(2,1)} %collective-permute-done.1.refs_1_, ...), custom_call_target="tpu_custom_call" | custom-call | tf_op jit(solution)/shard_map/grad_parts/pallas_call | solution.py:265
  122.1 2.5 %slice_bitcast_fusion = (bf16[4,80,640]{2,1,0:T(8,128)(2,1)}, bf16[4,80,640]{2,1,0:T(8,128)(2,1)}, bf16[4,80,640]{2,1,0:T(8,128)(2,1)}) fusion(bf16[4,4,80,640]{3,2,1,0:T(8,128)(2,1)} %get-tuple-element.30), kind=kLoop, calls=%fused_computation.45 | loop fusion | bytes 2457600 | tf_op jit(solution)/shard_map/squeeze | solution.py:344
  124.5 3.0 %collective-permute-start.13 = (bf16[4,80,640]{2,1,0:T(8,128)(2,1)}, bf16[4,80,640]{2,1,0:T(8,128)(2,1)}, u32[]{:S(2)}, u32[]{:S(2)}) collective-permute-start(bf16[4,80,640]{2,1,0:T(8,128)(2,1)} %get-tuple-element.51), channel_id=1, source_target_pairs={{0,16},{4,20},{8,24},{12,28},{16,0},{20,4},{24,8},{28,12},{32,48},... | collective-permute-start | bytes 1228808 | tf_op jit(solution)/shard_map/ppermute | solution.py:33
  132.8 2.8 %fusion.29 = bf16[512,640]{1,0:T(8,128)(2,1)S(1)} fusion(bf16[512,1280]{1,0:T(8,128)(2,1)S(1)} %copy-done.1, bf16[4,1280,640]{2,1,0:T(8,128)(2,1)} %bitcast.111, s32[]{:T(128)S(6)} %select_n.101), kind=kOutput, calls=%fused_computation.28 | convolution fusion | flops 839188480 | bytes 3604484 | tf_op jit(solution)/shard_map/dot_general | solution.py:351
  135.6 2.6 %fusion.35 = bf16[512,640]{1,0:T(8,128)(2,1)S(1)} fusion(bf16[512,1280]{1,0:T(8,128)(2,1)S(1)} %copy-done.1, bf16[4,1280,640]{2,1,0:T(8,128)(2,1)} %bitcast.112, s32[]{:T(128)S(6)} %select_n.105), kind=kOutput, calls=%fused_computation.30 | convolution fusion | flops 839188480 | bytes 3604484 | tf_op jit(solution)/shard_map/dot_general | solution.py:351
  147.8 2.3 %fusion.14 = f32[512,1280]{1,0:T(8,128)S(1)} fusion(bf16[512,640]{1,0:T(8,128)(2,1)} %collective-permute-done.2.refs_2_, bf16[4,1280,640]{2,1,0:T(8,128)(2,1)S(1)} %bitcast.116, s32[]{:T(128)S(6)} %select_n.99), kind=kOutput, calls=%fused_computation.15 | convolution fusion | flops 838860800 | bytes 4915204 | tf_op jit(solution)/shard_map/dot_general | solution.py:365
  154.6 2.6 %collective-permute-done.8 = bf16[4,80,640]{2,1,0:T(8,128)(2,1)S(1)} collective-permute-done((bf16[4,80,640]{2,1,0:T(8,128)(2,1)S(1)}, bf16[4,80,640]{2,1,0:T(8,128)(2,1)S(1)}, u32[]{:S(2)}, u32[]{:S(2)}) %collective-permute-start.8) | collective-permute-done | bytes 409632 | tf_op jit(solution)/shard_map/ppermute | solution.py:27
  157.2 2.7 %collective-permute-done.15 = bf16[512,640]{1,0:T(8,128)(2,1)S(1)} collective-permute-done((bf16[512,640]{1,0:T(8,128)(2,1)S(1)}, bf16[512,640]{1,0:T(8,128)(2,1)S(1)}, u32[]{:S(2)}, u32[]{:S(2)}) %collective-permute-start.15) | collective-permute-done | bytes 655392 | tf_op jit(solution)/shard_map/ppermute | solution.py:39
  165.2 3.0 %collective-permute-done.21 = bf16[80,640]{1,0:T(8,128)(2,1)S(1)} collective-permute-done((bf16[80,640]{1,0:T(8,128)(2,1)S(1)}, bf16[80,640]{1,0:T(8,128)(2,1)S(1)}, u32[]{:S(2)}, u32[]{:S(2)}) %collective-permute-start.21) | collective-permute-done | bytes 102432 | tf_op jit(solution)/shard_map/ppermute | solution.py:27
  168.8 2.5 %collective-permute-start.17 = (bf16[80,640]{1,0:T(8,128)(2,1)S(1)}, bf16[80,640]{1,0:T(8,128)(2,1)S(1)}, u32[]{:S(2)}, u32[]{:S(2)}) collective-permute-start(bf16[80,640]{1,0:T(8,128)(2,1)S(1)} %get-tuple-element.63), channel_id=1, source_target_pairs={{0,24},{4,28},{8,0},{12,4},{16,8},{20,12},{24,16},{28,20},{32,56},... | collective-permute-start | bytes 307208 | tf_op jit(solution)/shard_map/ppermute | solution.py:33
  171.3 2.3 %fusion.2 = bf16[512,1280]{1,0:T(8,128)(2,1)} fusion(f32[512,1280]{1,0:T(8,128)S(1)} %fusion.8, f32[512,1280]{1,0:T(8,128)S(1)} %fusion.14, f32[512,1280]{1,0:T(8,128)S(1)} %fusion.4, bf16[512,640]{1,0:T(8,128)(2,1)S(1)} %copy-done.3, bf16[4,1280,640]{2,1,0:T(8,128)(2,1)S(1)} %bitcast.118, s32[]{:T(128)S(6)} %select_n.107), kind=kOutput, calls=%fused_computation.3 | convolution fusion | flops 841482240 | bytes 11468804 | tf_op jit(solution)/shard_map/dot_general | solution.py:365
  174.8 2.4 %collective-permute-done.16 = bf16[80,640]{1,0:T(8,128)(2,1)S(1)} collective-permute-done((bf16[80,640]{1,0:T(8,128)(2,1)S(1)}, bf16[80,640]{1,0:T(8,128)(2,1)S(1)}, u32[]{:S(2)}, u32[]{:S(2)}) %collective-permute-start.16) | collective-permute-done | bytes 102432 | tf_op jit(solution)/shard_map/ppermute | solution.py:33
  177.3 5.2 %collective-permute-start.24 = (bf16[160,640]{1,0:T(8,128)(2,1)S(1)}, bf16[160,640]{1,0:T(8,128)(2,1)S(1)}, u32[]{:S(2)}, u32[]{:S(2)}) collective-permute-start(bf16[160,640]{1,0:T(8,128)(2,1)S(1)} %fusion.44), channel_id=1, source_target_pairs={{0,0},{1,32},{2,64},{3,96},{4,4},{5,36},{6,68},{7,100},{8,8},{9,40... | collective-permute-start | bytes 614408 | tf_op jit(solution)/shard_map/ppermute | solution.py:52
  183.7 8.1 %collective-permute-done.24 = bf16[160,640]{1,0:T(8,128)(2,1)S(1)} collective-permute-done((bf16[160,640]{1,0:T(8,128)(2,1)S(1)}, bf16[160,640]{1,0:T(8,128)(2,1)S(1)}, u32[]{:S(2)}, u32[]{:S(2)}) %collective-permute-start.24) | collective-permute-done | bytes 204832 | tf_op jit(solution)/shard_map/ppermute | solution.py:52
  (96 shorter events, 40.4 us)
Async XLA Ops:
  32.3 37.9 %all-to-all-start = ((bf16[32,40,640]{2,1,0:T(8,128)(2,1)}), bf16[32,40,640]{2,1,0:T(8,128)(2,1)S(1)}, u32[]{:S(2)}, u32[]{:S(2)}) async-start(bf16[32,40,640]{2,1,0:T(8,128)(2,1)} %pack.1), calls=%async_computation | async-start | bytes 3276800 | tf_op jit(solution)/shard_map/all_to_all | solution.py:324
  40.9 91.9 %all-gather.2.cloned.1.call-start = ((), (), s32[]{:S(2)}) async-start(), calls=%async_computation.1 | async-start | bytes 6758400 | tf_op jit(solution)/shard_map/all_gather | solution.py:328
  41.0 29.3 %collective-permute-start.14 = (bf16[160,640]{1,0:T(8,128)(2,1)S(1)}, bf16[160,640]{1,0:T(8,128)(2,1)S(1)}, u32[]{:S(2)}, u32[]{:S(2)}) collective-permute-start(bf16[160,640]{1,0:T(8,128)(2,1)S(1)} %copy-done.11), channel_id=1, source_target_pairs={{0,0},{1,32},{2,64},{3,96},{4,4},{5,36},{6,68},{7,100},{8,8},{9,40... | collective-permute-start | bytes 614408 | tf_op jit(solution)/shard_map/ppermute | solution.py:52
  77.2 29.7 %collective-permute-start.3 = (bf16[512,640]{1,0:T(8,128)(2,1)}, bf16[512,640]{1,0:T(8,128)(2,1)S(1)}, u32[]{:S(2)}, u32[]{:S(2)}) collective-permute-start(bf16[512,640]{1,0:T(8,128)(2,1)} %get-tuple-element.39.refs_0_), channel_id=1, source_target_pairs={{0,3},{1,0},{2,1},{3,2},{4,7},{5,4},{6,5},{7,6},{8,11},{9,8},{10,9... | collective-permute-start | bytes 1966088 | tf_op jit(solution)/shard_map/ppermute | solution.py:39
  79.0 27.9 %collective-permute-start.2 = (bf16[512,640]{1,0:T(8,128)(2,1)}, bf16[512,640]{1,0:T(8,128)(2,1)}, u32[]{:S(2)}, u32[]{:S(2)}) collective-permute-start(bf16[512,640]{1,0:T(8,128)(2,1)} %get-tuple-element.39.refs_0_), channel_id=1, source_target_pairs={{0,2},{1,3},{2,0},{3,1},{4,6},{5,7},{6,4},{7,5},{8,10},{9,11},{10,... | collective-permute-start | bytes 1966088 | tf_op jit(solution)/shard_map/ppermute | solution.py:39
  80.5 30.1 %collective-permute-start.1 = (bf16[512,640]{1,0:T(8,128)(2,1)}, bf16[512,640]{1,0:T(8,128)(2,1)}, u32[]{:S(2)}, u32[]{:S(2)}) collective-permute-start(bf16[512,640]{1,0:T(8,128)(2,1)} %get-tuple-element.39.refs_0_), channel_id=1, source_target_pairs={{0,1},{1,2},{2,3},{3,0},{4,5},{5,6},{6,7},{7,4},{8,9},{9,10},{10,1... | collective-permute-start | bytes 1966088 | tf_op jit(solution)/shard_map/ppermute | solution.py:39
  90.1 21.1 %collective-permute-start = (bf16[640,512]{1,0:T(8,128)(2,1)S(1)}, bf16[640,512]{1,0:T(8,128)(2,1)S(1)}, u32[]{:S(2)}, u32[]{:S(2)}) collective-permute-start(bf16[640,512]{1,0:T(8,128)(2,1)S(1)} %get-tuple-element.58), channel_id=1, source_target_pairs={{0,4},{4,0},{8,12},{12,8},{16,20},{20,16},{24,28},{28,24},{32,36},... | collective-permute-start | bytes 1966088 | tf_op jit(solution)/shard_map/ppermute | solution.py:43
  91.1 21.4 %collective-permute-start.4 = (bf16[512,640]{1,0:T(8,128)(2,1)S(1)}, bf16[512,640]{1,0:T(8,128)(2,1)}, u32[]{:S(2)}, u32[]{:S(2)}) collective-permute-start(bf16[512,640]{1,0:T(8,128)(2,1)S(1)} %copy-done.2), channel_id=1, source_target_pairs={{0,4},{4,0},{8,12},{12,8},{16,20},{20,16},{24,28},{28,24},{32,36},... | collective-permute-start | bytes 1966088 | tf_op jit(solution)/shard_map/ppermute | solution.py:43
  106.9 5.6 %collective-permute-start.7 = (bf16[512,640]{1,0:T(8,128)(2,1)S(1)}, bf16[512,640]{1,0:T(8,128)(2,1)}, u32[]{:S(2)}, u32[]{:S(2)}) collective-permute-start(bf16[512,640]{1,0:T(8,128)(2,1)S(1)} %collective-permute-done.3.refs_3_), channel_id=1, source_target_pairs={{0,4},{4,0},{8,12},{12,8},{16,20},{20,16},{24,28},{28,24},{32,36},... | collective-permute-start | bytes 1966088 | tf_op jit(solution)/shard_map/ppermute | solution.py:43
  124.5 19.2 %collective-permute-start.13 = (bf16[4,80,640]{2,1,0:T(8,128)(2,1)}, bf16[4,80,640]{2,1,0:T(8,128)(2,1)}, u32[]{:S(2)}, u32[]{:S(2)}) collective-permute-start(bf16[4,80,640]{2,1,0:T(8,128)(2,1)} %get-tuple-element.51), channel_id=1, source_target_pairs={{0,16},{4,20},{8,24},{12,28},{16,0},{20,4},{24,8},{28,12},{32,48},... | collective-permute-start | bytes 1228808 | tf_op jit(solution)/shard_map/ppermute | solution.py:33
  127.5 19.2 %collective-permute-start.12 = (bf16[4,80,640]{2,1,0:T(8,128)(2,1)}, bf16[4,80,640]{2,1,0:T(8,128)(2,1)}, u32[]{:S(2)}, u32[]{:S(2)}) collective-permute-start(bf16[4,80,640]{2,1,0:T(8,128)(2,1)} %get-tuple-element.52), channel_id=1, source_target_pairs={{0,24},{4,28},{8,0},{12,4},{16,8},{20,12},{24,16},{28,20},{32,56},... | collective-permute-start | bytes 1228808 | tf_op jit(solution)/shard_map/ppermute | solution.py:33
  128.9 22.4 %collective-permute-start.11 = (bf16[4,80,640]{2,1,0:T(8,128)(2,1)}, bf16[4,80,640]{2,1,0:T(8,128)(2,1)}, u32[]{:S(2)}, u32[]{:S(2)}) collective-permute-start(bf16[4,80,640]{2,1,0:T(8,128)(2,1)} %get-tuple-element.53), channel_id=1, source_target_pairs={{0,8},{4,12},{8,16},{12,20},{16,24},{20,28},{24,0},{28,4},{32,40},... | collective-permute-start | bytes 1228808 | tf_op jit(solution)/shard_map/ppermute | solution.py:33
  130.5 22.0 %collective-permute-start.10 = (bf16[4,80,640]{2,1,0:T(8,128)(2,1)}, bf16[4,80,640]{2,1,0:T(8,128)(2,1)}, u32[]{:S(2)}, u32[]{:S(2)}) collective-permute-start(bf16[4,80,640]{2,1,0:T(8,128)(2,1)} %get-tuple-element.54), channel_id=1, source_target_pairs={{0,64},{4,68},{8,72},{12,76},{16,80},{20,84},{24,88},{28,92},{32,9... | collective-permute-start | bytes 1228808 | tf_op jit(solution)/shard_map/ppermute | solution.py:27
  140.6 19.3 %collective-permute-start.15 = (bf16[512,640]{1,0:T(8,128)(2,1)S(1)}, bf16[512,640]{1,0:T(8,128)(2,1)S(1)}, u32[]{:S(2)}, u32[]{:S(2)}) collective-permute-start(bf16[512,640]{1,0:T(8,128)(2,1)S(1)} %fusion.26), channel_id=1, source_target_pairs={{0,2},{1,3},{2,0},{3,1},{4,6},{5,7},{6,4},{7,5},{8,10},{9,11},{10,... | collective-permute-start | bytes 1966088 | tf_op jit(solution)/shard_map/ppermute | solution.py:39
  143.8 10.9 %collective-permute-start.9 = (bf16[4,80,640]{2,1,0:T(8,128)(2,1)S(1)}, bf16[4,80,640]{2,1,0:T(8,128)(2,1)S(1)}, u32[]{:S(2)}, u32[]{:S(2)}) collective-permute-start(bf16[4,80,640]{2,1,0:T(8,128)(2,1)S(1)} %copy-done.7), channel_id=1, source_target_pairs={{0,96},{4,100},{8,104},{12,108},{16,112},{20,116},{24,120},{28,124... | collective-permute-start | bytes 1228808 | tf_op jit(solution)/shard_map/ppermute | solution.py:27
  146.7 10.5 %collective-permute-start.8 = (bf16[4,80,640]{2,1,0:T(8,128)(2,1)S(1)}, bf16[4,80,640]{2,1,0:T(8,128)(2,1)S(1)}, u32[]{:S(2)}, u32[]{:S(2)}) collective-permute-start(bf16[4,80,640]{2,1,0:T(8,128)(2,1)S(1)} %get-tuple-element.56), channel_id=1, source_target_pairs={{0,32},{4,36},{8,40},{12,44},{16,48},{20,52},{24,56},{28,60},{32,6... | collective-permute-start | bytes 1228808 | tf_op jit(solution)/shard_map/ppermute | solution.py:27
  151.3 31.3 %collective-permute-start.22 = (bf16[512,640]{1,0:T(8,128)(2,1)S(1)}, bf16[512,640]{1,0:T(8,128)(2,1)S(1)}, u32[]{:S(2)}, u32[]{:S(2)}) collective-permute-start(bf16[512,640]{1,0:T(8,128)(2,1)S(1)} %fusion.32), channel_id=1, source_target_pairs={{0,1},{1,2},{2,3},{3,0},{4,5},{5,6},{6,7},{7,4},{8,9},{9,10},{10,1... | collective-permute-start | bytes 1966088 | tf_op jit(solution)/shard_map/ppermute | solution.py:39
  152.6 30.0 %collective-permute-start.23 = (bf16[512,640]{1,0:T(8,128)(2,1)S(1)}, bf16[512,640]{1,0:T(8,128)(2,1)S(1)}, u32[]{:S(2)}, u32[]{:S(2)}) collective-permute-start(bf16[512,640]{1,0:T(8,128)(2,1)S(1)} %fusion.35), channel_id=1, source_target_pairs={{0,3},{1,0},{2,1},{3,2},{4,7},{5,4},{6,5},{7,6},{8,11},{9,8},{10,9... | collective-permute-start | bytes 1966088 | tf_op jit(solution)/shard_map/ppermute | solution.py:39
  161.9 6.3 %collective-permute-start.21 = (bf16[80,640]{1,0:T(8,128)(2,1)S(1)}, bf16[80,640]{1,0:T(8,128)(2,1)S(1)}, u32[]{:S(2)}, u32[]{:S(2)}) collective-permute-start(bf16[80,640]{1,0:T(8,128)(2,1)S(1)} %get-tuple-element.59), channel_id=1, source_target_pairs={{0,64},{4,68},{8,72},{12,76},{16,80},{20,84},{24,88},{28,92},{32,9... | collective-permute-start | bytes 307208 | tf_op jit(solution)/shard_map/ppermute | solution.py:27
  163.2 8.1 %collective-permute-start.19 = (bf16[80,640]{1,0:T(8,128)(2,1)S(1)}, bf16[80,640]{1,0:T(8,128)(2,1)S(1)}, u32[]{:S(2)}, u32[]{:S(2)}) collective-permute-start(bf16[80,640]{1,0:T(8,128)(2,1)S(1)} %get-tuple-element.61), channel_id=1, source_target_pairs={{0,32},{4,36},{8,40},{12,44},{16,48},{20,52},{24,56},{28,60},{32,6... | collective-permute-start | bytes 307208 | tf_op jit(solution)/shard_map/ppermute | solution.py:27
  168.2 6.3 %collective-permute-start.18 = (bf16[80,640]{1,0:T(8,128)(2,1)S(1)}, bf16[80,640]{1,0:T(8,128)(2,1)S(1)}, u32[]{:S(2)}, u32[]{:S(2)}) collective-permute-start(bf16[80,640]{1,0:T(8,128)(2,1)S(1)} %get-tuple-element.62), channel_id=1, source_target_pairs={{0,16},{4,20},{8,24},{12,28},{16,0},{20,4},{24,8},{28,12},{32,48},... | collective-permute-start | bytes 307208 | tf_op jit(solution)/shard_map/ppermute | solution.py:33
  168.8 6.0 %collective-permute-start.17 = (bf16[80,640]{1,0:T(8,128)(2,1)S(1)}, bf16[80,640]{1,0:T(8,128)(2,1)S(1)}, u32[]{:S(2)}, u32[]{:S(2)}) collective-permute-start(bf16[80,640]{1,0:T(8,128)(2,1)S(1)} %get-tuple-element.63), channel_id=1, source_target_pairs={{0,24},{4,28},{8,0},{12,4},{16,8},{20,12},{24,16},{28,20},{32,56},... | collective-permute-start | bytes 307208 | tf_op jit(solution)/shard_map/ppermute | solution.py:33
  171.3 5.9 %collective-permute-start.16 = (bf16[80,640]{1,0:T(8,128)(2,1)S(1)}, bf16[80,640]{1,0:T(8,128)(2,1)S(1)}, u32[]{:S(2)}, u32[]{:S(2)}) collective-permute-start(bf16[80,640]{1,0:T(8,128)(2,1)S(1)} %get-tuple-element.64), channel_id=1, source_target_pairs={{0,8},{4,12},{8,16},{12,20},{16,24},{20,28},{24,0},{28,4},{32,40},... | collective-permute-start | bytes 307208 | tf_op jit(solution)/shard_map/ppermute | solution.py:33
  177.3 14.5 %collective-permute-start.24 = (bf16[160,640]{1,0:T(8,128)(2,1)S(1)}, bf16[160,640]{1,0:T(8,128)(2,1)S(1)}, u32[]{:S(2)}, u32[]{:S(2)}) collective-permute-start(bf16[160,640]{1,0:T(8,128)(2,1)S(1)} %fusion.44), channel_id=1, source_target_pairs={{0,0},{1,32},{2,64},{3,96},{4,4},{5,36},{6,68},{7,100},{8,8},{9,40... | collective-permute-start | bytes 614408 | tf_op jit(solution)/shard_map/ppermute | solution.py:52
  (17 other events, 98.7 us)
Sparse Core Ops, SparseCore 0:
  71.1 49.3 all-gather.1

commit v3 on v2

--- a/solution.py
+++ b/solution.py
@@ -240,17 +240,24 @@
     )(got, word, cotangent)
 
 
-def grad_kernel(where_ref, left_ref, *refs):
-    mine, theirs, (a_ref, b_ref) = refs[:4], refs[4:8], refs[8:]
+def grad_kernel(where_ref, left_ref, *refs, shifts, kept):
+    count = len(shifts)
+    mine, theirs, old = refs[:count], refs[count : 2 * count], refs[2 * count : -2]
+    a_ref, b_ref = refs[-2:]
     tokens = mine[0].shape[0]
     x, z, y = where_ref[0], where_ref[1], where_ref[2]
     half = left_ref.shape[0] // 2
     step = half // NZ
-    for i in range(NY):
+    for i in kept:
+        xs = lax.rem(y - i - x + 2 * NX, NX)
+        a_ref[xs] = old[0][xs]
+        for k in range(NZ):
+            b_ref[k, xs] = old[1][k, xs]
+    for n, i in enumerate(shifts):
         xs = lax.rem(y - i - x + 2 * NX, NX)
         left = left_ref[...]
-        got = jnp.dot(left[:, :tokens], mine[i][...], preferred_element_type=F32)
-        got = got + jnp.dot(left[:, tokens:], theirs[i][...], preferred_element_type=F32)
+        got = jnp.dot(left[:, :tokens], mine[n][...], preferred_element_type=F32)
+        got = got + jnp.dot(left[:, tokens:], theirs[n][...], preferred_element_type=F32)
         got = got.astype(BF)
         for k in range(NZ):
             zs = lax.rem(k - z + NZ, NZ)
@@ -258,21 +265,21 @@
             b_ref[zs, xs] = got[half + k * step : half + (k + 1) * step]
 
 
-def grad_parts(where, left, mine, theirs):
+def grad_parts(where, left, mine, theirs, shifts, kept=(), old=()):
     width = mine[0].shape[1]
     step = left.shape[0] // 2 // NZ
     shape = jax.ShapeDtypeStruct((4, 4, step, width), BF)
     return pl.pallas_call(
-        grad_kernel,
+        functools.partial(grad_kernel, shifts=shifts, kept=kept),
         out_shape=(shape, shape),
         in_specs=[pl.BlockSpec(memory_space=pltpu.SMEM)]
-        + [pl.BlockSpec(memory_space=pltpu.VMEM)] * 9,
+        + [pl.BlockSpec(memory_space=pltpu.VMEM)] * (1 + 2 * len(shifts) + len(old)),
         out_specs=(
             pl.BlockSpec(memory_space=pltpu.VMEM),
             pl.BlockSpec(memory_space=pltpu.VMEM),
         ),
         name="grad_parts",
-    )(where, left, *mine, *theirs)
+    )(where, left, *mine, *theirs, *old)
 
 
 def total(*parts):
@@ -328,7 +335,10 @@
     weight = lax.all_gather(weight_tile, "dp", axis=0, tiled=True)
     weight = weight.reshape(NX, -1, feat_width)
 
-    mine = [acts] + [along_y(acts, s) for s in (1, 2, 3)]
+    below, above = along_y(acts, 1), along_y(acts, 3)
+    middle = tokens // 2
+    far = jnp.concatenate([along_y(below[:middle], 1), along_y(above[middle:], 3)], axis=0)
+    mine = [acts, below, far, above]
     theirs = [to_partner(block_cols) for block_cols in mine]
 
     signal = weigh(got_rows, word, cotangent)
@@ -339,7 +349,9 @@
     left = jnp.concatenate([own_side, to_partner(other_side)], axis=1)
 
     where = jnp.stack([x, z, y])
-    part_a, part_b = grad_parts(where, left, mine, theirs)
+    near = (0, 1, 3)
+    early = grad_parts(where, left, [mine[i] for i in near], [theirs[i] for i in near], near)
+    part_a, part_b = grad_parts(where, left, [far], [theirs[2]], (2,), near, early)
     more_a = [along_x(part_a[s], s) for s in (1, 3, 2)]
     more_b = [along_z(part_b[s], s) for s in (1, 3, 2)]
 

time: 200 us -> 205 us (1.025)
  waiting for transfers between devices: 65.7 us -> 58.3 us
  starting transfers between devices: 42.5 us -> 48.4 us
  Pallas kernels: 46 us -> 50.1 us
  local copies, waits for them, and re-layouts: 8.98 us -> 12.7 us
  matrix products: 15.9 us -> 13.7 us
    ppermute x6 -> x7, waiting for transfers between devices: 21.6 us -> 15.4 us  [along_y(): return lax.ppermute(value, 'mp', [(y, (y + shift) % NY) for y in range(NY)])]
    pallas_call x1 -> x2, Pallas kernels: 9.07 us -> 13.3 us  [grad_parts(): pl.pallas_call(functools.partial(grad_kernel, shifts=shifts, kept=kept),...]
    ppermute x6, starting transfers between devices: 7.79 us -> 12 us  [along_x(): lax.ppermute(value, 'dp', [(place(x, z, c), place(x + shift, z, c)) for x...]
    ppermute x6 -> x7, starting transfers between devices: 7.41 us -> 10 us  [along_y(): return lax.ppermute(value, 'mp', [(y, (y + shift) % NY) for y in range(NY)])]
    dot_general x4, matrix products: 8.13 us -> 5.98 us  [local(): lax.dot_general(mine[s], columns(y - s + NY), (((1,), (1,)), ((), ())), p...]
  transfers between devices with their start and end apart: 27 -> 28, of which waited for: 12 -> 10; matrix products, arithmetic and copies ran while one was open for 13% -> 14% of each run, Pallas kernels for 11% -> 13%
where the time goes in v3:
time: 205 us; the launch traced here: 204 us
  waiting for transfers between devices  58.3 us (28%)
  Pallas kernels  50.1 us (24%)
  starting transfers between devices  48.4 us (24%)
  between operations  14.4 us (7%)
  matrix products  13.7 us (7%)
  local copies, waits for them, and re-layouts  12.7 us (6%)
  other arithmetic  6 us (3%)
    ppermute x2, waiting for transfers between devices, swap_xy(): return lax.ppermute(value, ('dp', 'mp'), pairs)  31.6 us
    pallas_call x2, Pallas kernels, attend(): pl.pallas_call(functools.partial(attend_kernel, first=first), out_shape=j...  19.7 us
    ppermute x7, waiting for transfers between devices, along_y(): return lax.ppermute(value, 'mp', [(y, (y + shift) % NY) for y in range(NY)])  15.4 us
    pallas_call x2, Pallas kernels, grad_parts(): pl.pallas_call(functools.partial(grad_kernel, shifts=shifts, kept=kept),...  13.3 us
    ppermute x6, starting transfers between devices, along_x(): lax.ppermute(value, 'dp', [(place(x, z, c), place(x + shift, z, c)) for x...  12 us
    ppermute x7, starting transfers between devices, along_y(): return lax.ppermute(value, 'mp', [(y, (y + shift) % NY) for y in range(NY)])  10 us
    ppermute x6, starting transfers between devices, along_z(): lax.ppermute(value, 'dp', [(place(x, z, c), place(x, z + shift, c)) for x...  8.61 us
    all_to_all x1, starting transfers between devices, local(): lax.all_to_all(send_rows, 'dp', split_axis=0, concat_axis=0, tiled=True)  8.58 us
  transfers between devices with their start and end apart: 28, of which 10 were waited for; matrix products, arithmetic and copies ran while one was open for 14% of the time, Pallas kernels for 13%

profile of v3, /device:TPU:4, one launch (start us, length us, event | category | flops | bytes accessed | tf_op | source)
XLA Modules:
  0.0 203.7 jit_solution(1968447452541610276)
XLA Ops:
  7.2 9.8 %attend.3.b_ref = bf16[256,640]{1,0:T(8,128)(2,1)} custom-call(s32[128]{0:T(128)} %lengths_ref.3, bf16[128,4,640]{2,1,0:T(4,128)(2,1)} %q_ref.3, bf16[512,128]{1,0:T(8,128)(2,1)} %bitcast.107, bf16[512,128]{1,0:T(8,128)(2,1)} %bitcast.109, bf16[128,256,128]{2,1,0:T(8,128)(2,1)} %k_ref.3, bf16[128,256,128]{2,1,0:T(8,128)(2,1)} %v_ref.3), custom_call_target="tpu_custom_call" | custom-call | tf_op jit(solution)/shard_map/attend/pallas_call | solution.py:116
  17.0 9.9 %attend.2.a_ref = bf16[256,640]{1,0:T(8,128)(2,1)} custom-call(s32[128]{0:T(128)} %lengths_ref.3, bf16[128,4,640]{2,1,0:T(4,128)(2,1)} %q_ref.3, bf16[512,128]{1,0:T(8,128)(2,1)} %bitcast.108, bf16[512,128]{1,0:T(8,128)(2,1)} %bitcast.110, bf16[128,256,128]{2,1,0:T(8,128)(2,1)} %k_ref.3, bf16[128,256,128]{2,1,0:T(8,128)(2,1)} %v_ref.3), custom_call_target="tpu_custom_call" | custom-call | tf_op jit(solution)/shard_map/attend/pallas_call | solution.py:116
  28.5 3.8 %pack.1 = bf16[32,40,640]{2,1,0:T(8,128)(2,1)} custom-call(s32[1,512]{1,0:T(1,128)} %add.177.goes_ref, bf16[8,640]{1,0:T(8,128)(2,1)} %convert_convert_fusion.facts_ref, bf16[256,640]{1,0:T(8,128)(2,1)} %attend.2.a_ref, bf16[256,640]{1,0:T(8,128)(2,1)} %attend.3.b_ref), custom_call_target="tpu_custom_call" | custom-call | tf_op jit(solution)/shard_map/pack/pallas_call | solution.py:153
  32.3 8.6 %all-to-all-start = ((bf16[32,40,640]{2,1,0:T(8,128)(2,1)}), bf16[32,40,640]{2,1,0:T(8,128)(2,1)S(1)}, u32[]{:S(2)}, u32[]{:S(2)}) async-start(bf16[32,40,640]{2,1,0:T(8,128)(2,1)} %pack.1), calls=%async_computation | async-start | bytes 3276800 | tf_op jit(solution)/shard_map/all_to_all | solution.py:331
  41.0 4.8 %collective-permute-start.15 = (bf16[160,640]{1,0:T(8,128)(2,1)S(1)}, bf16[160,640]{1,0:T(8,128)(2,1)S(1)}, u32[]{:S(2)}, u32[]{:S(2)}) collective-permute-start(bf16[160,640]{1,0:T(8,128)(2,1)S(1)} %copy-done.14), channel_id=1, source_target_pairs={{0,0},{1,32},{2,64},{3,96},{4,4},{5,36},{6,68},{7,100},{8,8},{9,40... | collective-permute-start | bytes 614408 | tf_op jit(solution)/shard_map/ppermute | solution.py:52
  45.8 24.5 %collective-permute-done.15 = bf16[160,640]{1,0:T(8,128)(2,1)S(1)} collective-permute-done((bf16[160,640]{1,0:T(8,128)(2,1)S(1)}, bf16[160,640]{1,0:T(8,128)(2,1)S(1)}, u32[]{:S(2)}, u32[]{:S(2)}) %collective-permute-start.15) | collective-permute-done | bytes 204832 | tf_op jit(solution)/shard_map/ppermute | solution.py:52
  71.6 5.6 %unpack.1 = (bf16[512,640]{1,0:T(8,128)(2,1)}, s32[512,1]{1,0:T(8,128)}) custom-call(s32[1]{0:T(128)} %bitcast.11.block_ref, bf16[32,40,640]{2,1,0:T(8,128)(2,1)} %copy-done, bf16[1280,640]{1,0:T(8,128)(2,1)} %bitcast.103), custom_call_target="tpu_custom_call" | custom-call | tf_op jit(solution)/shard_map/unpack/pallas_call | solution.py:187
  80.4 14.1 %collective-permute-done.1.refs_1_ = bf16[512,640]{1,0:T(8,128)(2,1)S(1)} collective-permute-done((bf16[512,640]{1,0:T(8,128)(2,1)}, bf16[512,640]{1,0:T(8,128)(2,1)S(1)}, u32[]{:S(2)}, u32[]{:S(2)}) %collective-permute-start.1) | collective-permute-done | bytes 655392 | tf_op jit(solution)/shard_map/ppermute | solution.py:39
  96.6 2.9 %collective-permute-start.4 = (bf16[256,640]{1,0:T(8,128)(2,1)}, bf16[256,640]{1,0:T(8,128)(2,1)}, u32[]{:S(2)}, u32[]{:S(2)}) collective-permute-start(bf16[256,640]{1,0:T(8,128)(2,1)} %slice.73), channel_id=1, source_target_pairs={{0,3},{1,0},{2,1},{3,2},{4,7},{5,4},{6,5},{7,6},{8,11},{9,8},{10,9... | collective-permute-start | bytes 983048 | tf_op jit(solution)/shard_map/ppermute | solution.py:39
  99.5 7.7 %weigh.1 = bf16[512,1280]{1,0:T(8,128)(2,1)} custom-call(bf16[32,40,640]{2,1,0:T(8,128)(2,1)} %copy-done, s32[512,1]{1,0:T(8,128)} %get-tuple-element.29.word_ref, bf16[512,1280]{1,0:T(8,128)(2,1)} %cot_ref.1), custom_call_target="tpu_custom_call" | custom-call | tf_op jit(solution)/shard_map/weigh/pallas_call | solution.py:229
  115.2 7.6 %grad_parts.2 = (bf16[4,4,80,640]{3,2,1,0:T(8,128)(2,1)}, bf16[4,4,80,640]{3,2,1,0:T(8,128)(2,1)}) custom-call(s32[3]{0:T(128)} %pad_add_fusion.where_ref, bf16[640,1024]{1,0:T(8,128)(2,1)} %pad_maximum_fusion.left_ref, bf16[512,640]{1,0:T(8,128)(2,1)} %get-tuple-element.43.refs_0_, bf16[512,640]{1,0:T(8,128)(2,1)} %copy-done.8, bf16[512,640]{1,0:T(8,128)(2,1)} %copy-done.6, ...), custom_call_target="tpu_custom_call" | custom-call | tf_op jit(solution)/shard_map/grad_parts/pallas_call | solution.py:272
  122.7 5.7 %grad_parts.3 = (bf16[4,4,80,640]{3,2,1,0:T(8,128)(2,1)}, bf16[4,4,80,640]{3,2,1,0:T(8,128)(2,1)}) custom-call(s32[3]{0:T(128)} %pad_add_fusion.where_ref, bf16[640,1024]{1,0:T(8,128)(2,1)} %pad_maximum_fusion.left_ref, bf16[512,640]{1,0:T(8,128)(2,1)} %copy-done.4, bf16[512,640]{1,0:T(8,128)(2,1)} %collective-permute-done.5.refs_1_, ...), custom_call_target="tpu_custom_call" | custom-call | tf_op jit(solution)/shard_map/grad_parts/pallas_call | solution.py:272
  130.9 2.6 %collective-permute-start.14 = (bf16[4,80,640]{2,1,0:T(8,128)(2,1)}, bf16[4,80,640]{2,1,0:T(8,128)(2,1)}, u32[]{:S(2)}, u32[]{:S(2)}) collective-permute-start(bf16[4,80,640]{2,1,0:T(8,128)(2,1)} %get-tuple-element.55), channel_id=1, source_target_pairs={{0,16},{4,20},{8,24},{12,28},{16,0},{20,4},{24,8},{28,12},{32,48},... | collective-permute-start | bytes 1228808 | tf_op jit(solution)/shard_map/ppermute | solution.py:33
  138.4 2.8 %fusion.29 = bf16[512,640]{1,0:T(8,128)(2,1)S(1)} fusion(bf16[512,1280]{1,0:T(8,128)(2,1)S(1)} %copy-done.1, bf16[4,1280,640]{2,1,0:T(8,128)(2,1)} %bitcast.111, s32[]{:T(128)S(6)} %select_n.101), kind=kOutput, calls=%fused_computation.28 | convolution fusion | flops 839188480 | bytes 3604484 | tf_op jit(solution)/shard_map/dot_general | solution.py:363
  141.2 2.6 %fusion.35 = bf16[512,640]{1,0:T(8,128)(2,1)S(1)} fusion(bf16[512,1280]{1,0:T(8,128)(2,1)S(1)} %copy-done.1, bf16[4,1280,640]{2,1,0:T(8,128)(2,1)} %bitcast.112, s32[]{:T(128)S(6)} %select_n.105), kind=kOutput, calls=%fused_computation.30 | convolution fusion | flops 839188480 | bytes 3604484 | tf_op jit(solution)/shard_map/dot_general | solution.py:363
  147.7 2.5 %collective-permute-start.10 = (bf16[4,80,640]{2,1,0:T(8,128)(2,1)S(1)}, bf16[4,80,640]{2,1,0:T(8,128)(2,1)S(1)}, u32[]{:S(2)}, u32[]{:S(2)}) collective-permute-start(bf16[4,80,640]{2,1,0:T(8,128)(2,1)S(1)} %copy-done.10), channel_id=1, source_target_pairs={{0,96},{4,100},{8,104},{12,108},{16,112},{20,116},{24,120},{28,124... | collective-permute-start | bytes 1228808 | tf_op jit(solution)/shard_map/ppermute | solution.py:27
  150.3 2.8 %collective-permute-done.13 = bf16[4,80,640]{2,1,0:T(8,128)(2,1)} collective-permute-done((bf16[4,80,640]{2,1,0:T(8,128)(2,1)}, bf16[4,80,640]{2,1,0:T(8,128)(2,1)}, u32[]{:S(2)}, u32[]{:S(2)}) %collective-permute-start.13) | collective-permute-done | bytes 409632 | tf_op jit(solution)/shard_map/ppermute | solution.py:33
  153.1 2.8 %collective-permute-start.9 = (bf16[4,80,640]{2,1,0:T(8,128)(2,1)S(1)}, bf16[4,80,640]{2,1,0:T(8,128)(2,1)S(1)}, u32[]{:S(2)}, u32[]{:S(2)}) collective-permute-start(bf16[4,80,640]{2,1,0:T(8,128)(2,1)S(1)} %get-tuple-element.60), channel_id=1, source_target_pairs={{0,32},{4,36},{8,40},{12,44},{16,48},{20,52},{24,56},{28,60},{32,6... | collective-permute-start | bytes 1228808 | tf_op jit(solution)/shard_map/ppermute | solution.py:27
  158.4 3.2 %collective-permute-start.24 = (bf16[512,640]{1,0:T(8,128)(2,1)S(1)}, bf16[512,640]{1,0:T(8,128)(2,1)S(1)}, u32[]{:S(2)}, u32[]{:S(2)}) collective-permute-start(bf16[512,640]{1,0:T(8,128)(2,1)S(1)} %fusion.35), channel_id=1, source_target_pairs={{0,3},{1,0},{2,1},{3,2},{4,7},{5,4},{6,5},{7,6},{8,11},{9,8},{10,9... | collective-permute-start | bytes 1966088 | tf_op jit(solution)/shard_map/ppermute | solution.py:39
  161.6 2.6 %collective-permute-done.9 = bf16[4,80,640]{2,1,0:T(8,128)(2,1)S(1)} collective-permute-done((bf16[4,80,640]{2,1,0:T(8,128)(2,1)S(1)}, bf16[4,80,640]{2,1,0:T(8,128)(2,1)S(1)}, u32[]{:S(2)}, u32[]{:S(2)}) %collective-permute-start.9) | collective-permute-done | bytes 409632 | tf_op jit(solution)/shard_map/ppermute | solution.py:27
  176.0 2.6 %collective-permute-start.18 = (bf16[80,640]{1,0:T(8,128)(2,1)S(1)}, bf16[80,640]{1,0:T(8,128)(2,1)S(1)}, u32[]{:S(2)}, u32[]{:S(2)}) collective-permute-start(bf16[80,640]{1,0:T(8,128)(2,1)S(1)} %get-tuple-element.67), channel_id=1, source_target_pairs={{0,24},{4,28},{8,0},{12,4},{16,8},{20,12},{24,16},{28,20},{32,56},... | collective-permute-start | bytes 307208 | tf_op jit(solution)/shard_map/ppermute | solution.py:33
  181.1 3.3 %collective-permute-done.17 = bf16[80,640]{1,0:T(8,128)(2,1)S(1)} collective-permute-done((bf16[80,640]{1,0:T(8,128)(2,1)S(1)}, bf16[80,640]{1,0:T(8,128)(2,1)S(1)}, u32[]{:S(2)}, u32[]{:S(2)}) %collective-permute-start.17) | collective-permute-done | bytes 102432 | tf_op jit(solution)/shard_map/ppermute | solution.py:33
  184.6 3.3 %collective-permute-start.25 = (bf16[160,640]{1,0:T(8,128)(2,1)S(1)}, bf16[160,640]{1,0:T(8,128)(2,1)S(1)}, u32[]{:S(2)}, u32[]{:S(2)}) collective-permute-start(bf16[160,640]{1,0:T(8,128)(2,1)S(1)} %fusion.44), channel_id=1, source_target_pairs={{0,0},{1,32},{2,64},{3,96},{4,4},{5,36},{6,68},{7,100},{8,8},{9,40... | collective-permute-start | bytes 614408 | tf_op jit(solution)/shard_map/ppermute | solution.py:52
  189.1 7.1 %collective-permute-done.25 = bf16[160,640]{1,0:T(8,128)(2,1)S(1)} collective-permute-done((bf16[160,640]{1,0:T(8,128)(2,1)S(1)}, bf16[160,640]{1,0:T(8,128)(2,1)S(1)}, u32[]{:S(2)}, u32[]{:S(2)}) %collective-permute-start.25) | collective-permute-done | bytes 204832 | tf_op jit(solution)/shard_map/ppermute | solution.py:52
  (109 shorter events, 46.1 us)
Async XLA Ops:
  32.3 37.9 %all-to-all-start = ((bf16[32,40,640]{2,1,0:T(8,128)(2,1)}), bf16[32,40,640]{2,1,0:T(8,128)(2,1)S(1)}, u32[]{:S(2)}, u32[]{:S(2)}) async-start(bf16[32,40,640]{2,1,0:T(8,128)(2,1)} %pack.1), calls=%async_computation | async-start | bytes 3276800 | tf_op jit(solution)/shard_map/all_to_all | solution.py:331
  40.9 97.5 %all-gather.2.cloned.1.call-start = ((), (), s32[]{:S(2)}) async-start(), calls=%async_computation.1 | async-start | bytes 6758400 | tf_op jit(solution)/shard_map/all_gather | solution.py:335
  41.0 29.3 %collective-permute-start.15 = (bf16[160,640]{1,0:T(8,128)(2,1)S(1)}, bf16[160,640]{1,0:T(8,128)(2,1)S(1)}, u32[]{:S(2)}, u32[]{:S(2)}) collective-permute-start(bf16[160,640]{1,0:T(8,128)(2,1)S(1)} %copy-done.14), channel_id=1, source_target_pairs={{0,0},{1,32},{2,64},{3,96},{4,4},{5,36},{6,68},{7,100},{8,8},{9,40... | collective-permute-start | bytes 614408 | tf_op jit(solution)/shard_map/ppermute | solution.py:52
  77.2 17.4 %collective-permute-start.1 = (bf16[512,640]{1,0:T(8,128)(2,1)}, bf16[512,640]{1,0:T(8,128)(2,1)S(1)}, u32[]{:S(2)}, u32[]{:S(2)}) collective-permute-start(bf16[512,640]{1,0:T(8,128)(2,1)} %get-tuple-element.43.refs_0_), channel_id=1, source_target_pairs={{0,1},{1,2},{2,3},{3,0},{4,5},{5,6},{6,7},{7,4},{8,9},{9,10},{10,1... | collective-permute-start | bytes 1966088 | tf_op jit(solution)/shard_map/ppermute | solution.py:39
  78.4 17.3 %collective-permute-start.3 = (bf16[512,640]{1,0:T(8,128)(2,1)}, bf16[512,640]{1,0:T(8,128)(2,1)S(1)}, u32[]{:S(2)}, u32[]{:S(2)}) collective-permute-start(bf16[512,640]{1,0:T(8,128)(2,1)} %get-tuple-element.43.refs_0_), channel_id=1, source_target_pairs={{0,3},{1,0},{2,1},{3,2},{4,7},{5,4},{6,5},{7,6},{8,11},{9,8},{10,9... | collective-permute-start | bytes 1966088 | tf_op jit(solution)/shard_map/ppermute | solution.py:39
  95.4 15.1 %collective-permute-start.2 = (bf16[256,640]{1,0:T(8,128)(2,1)}, bf16[256,640]{1,0:T(8,128)(2,1)}, u32[]{:S(2)}, u32[]{:S(2)}) collective-permute-start(bf16[256,640]{1,0:T(8,128)(2,1)} %slice.72), channel_id=1, source_target_pairs={{0,1},{1,2},{2,3},{3,0},{4,5},{5,6},{6,7},{7,4},{8,9},{9,10},{10,1... | collective-permute-start | bytes 983048 | tf_op jit(solution)/shard_map/ppermute | solution.py:39
  96.6 15.4 %collective-permute-start.4 = (bf16[256,640]{1,0:T(8,128)(2,1)}, bf16[256,640]{1,0:T(8,128)(2,1)}, u32[]{:S(2)}, u32[]{:S(2)}) collective-permute-start(bf16[256,640]{1,0:T(8,128)(2,1)} %slice.73), channel_id=1, source_target_pairs={{0,3},{1,0},{2,1},{3,2},{4,7},{5,4},{6,5},{7,6},{8,11},{9,8},{10,9... | collective-permute-start | bytes 983048 | tf_op jit(solution)/shard_map/ppermute | solution.py:39
  99.4 15.7 %collective-permute-start.6 = (bf16[512,640]{1,0:T(8,128)(2,1)}, bf16[512,640]{1,0:T(8,128)(2,1)}, u32[]{:S(2)}, u32[]{:S(2)}) collective-permute-start(bf16[512,640]{1,0:T(8,128)(2,1)} %get-tuple-element.43.refs_0_), channel_id=1, source_target_pairs={{0,4},{4,0},{8,12},{12,8},{16,20},{20,16},{24,28},{28,24},{32,36},... | collective-permute-start | bytes 1966088 | tf_op jit(solution)/shard_map/ppermute | solution.py:43
  113.0 9.7 %collective-permute-start.5 = (bf16[512,640]{1,0:T(8,128)(2,1)S(1)}, bf16[512,640]{1,0:T(8,128)(2,1)}, u32[]{:S(2)}, u32[]{:S(2)}) collective-permute-start(bf16[512,640]{1,0:T(8,128)(2,1)S(1)} %constant_dynamic-update-slice_fusion.refs_0_), channel_id=1, source_target_pairs={{0,4},{4,0},{8,12},{12,8},{16,20},{20,16},{24,28},{28,24},{32,36},... | collective-permute-start | bytes 1966088 | tf_op jit(solution)/shard_map/ppermute | solution.py:43
  130.9 16.8 %collective-permute-start.14 = (bf16[4,80,640]{2,1,0:T(8,128)(2,1)}, bf16[4,80,640]{2,1,0:T(8,128)(2,1)}, u32[]{:S(2)}, u32[]{:S(2)}) collective-permute-start(bf16[4,80,640]{2,1,0:T(8,128)(2,1)} %get-tuple-element.55), channel_id=1, source_target_pairs={{0,16},{4,20},{8,24},{12,28},{16,0},{20,4},{24,8},{28,12},{32,48},... | collective-permute-start | bytes 1228808 | tf_op jit(solution)/shard_map/ppermute | solution.py:33
  133.5 19.6 %collective-permute-start.13 = (bf16[4,80,640]{2,1,0:T(8,128)(2,1)}, bf16[4,80,640]{2,1,0:T(8,128)(2,1)}, u32[]{:S(2)}, u32[]{:S(2)}) collective-permute-start(bf16[4,80,640]{2,1,0:T(8,128)(2,1)} %get-tuple-element.56), channel_id=1, source_target_pairs={{0,24},{4,28},{8,0},{12,4},{16,8},{20,12},{24,16},{28,20},{32,56},... | collective-permute-start | bytes 1228808 | tf_op jit(solution)/shard_map/ppermute | solution.py:33
  135.0 23.3 %collective-permute-start.12 = (bf16[4,80,640]{2,1,0:T(8,128)(2,1)}, bf16[4,80,640]{2,1,0:T(8,128)(2,1)}, u32[]{:S(2)}, u32[]{:S(2)}) collective-permute-start(bf16[4,80,640]{2,1,0:T(8,128)(2,1)} %get-tuple-element.57), channel_id=1, source_target_pairs={{0,8},{4,12},{8,16},{12,20},{16,24},{20,28},{24,0},{28,4},{32,40},... | collective-permute-start | bytes 1228808 | tf_op jit(solution)/shard_map/ppermute | solution.py:33
  136.5 21.9 %collective-permute-start.11 = (bf16[4,80,640]{2,1,0:T(8,128)(2,1)}, bf16[4,80,640]{2,1,0:T(8,128)(2,1)}, u32[]{:S(2)}, u32[]{:S(2)}) collective-permute-start(bf16[4,80,640]{2,1,0:T(8,128)(2,1)} %get-tuple-element.58), channel_id=1, source_target_pairs={{0,64},{4,68},{8,72},{12,76},{16,80},{20,84},{24,88},{28,92},{32,9... | collective-permute-start | bytes 1228808 | tf_op jit(solution)/shard_map/ppermute | solution.py:27
  146.3 19.3 %collective-permute-start.16 = (bf16[512,640]{1,0:T(8,128)(2,1)S(1)}, bf16[512,640]{1,0:T(8,128)(2,1)S(1)}, u32[]{:S(2)}, u32[]{:S(2)}) collective-permute-start(bf16[512,640]{1,0:T(8,128)(2,1)S(1)} %fusion.26), channel_id=1, source_target_pairs={{0,2},{1,3},{2,0},{3,1},{4,6},{5,7},{6,4},{7,5},{8,10},{9,11},{10,... | collective-permute-start | bytes 1966088 | tf_op jit(solution)/shard_map/ppermute | solution.py:39
  147.7 13.9 %collective-permute-start.10 = (bf16[4,80,640]{2,1,0:T(8,128)(2,1)S(1)}, bf16[4,80,640]{2,1,0:T(8,128)(2,1)S(1)}, u32[]{:S(2)}, u32[]{:S(2)}) collective-permute-start(bf16[4,80,640]{2,1,0:T(8,128)(2,1)S(1)} %copy-done.10), channel_id=1, source_target_pairs={{0,96},{4,100},{8,104},{12,108},{16,112},{20,116},{24,120},{28,124... | collective-permute-start | bytes 1228808 | tf_op jit(solution)/shard_map/ppermute | solution.py:27
  153.1 11.2 %collective-permute-start.9 = (bf16[4,80,640]{2,1,0:T(8,128)(2,1)S(1)}, bf16[4,80,640]{2,1,0:T(8,128)(2,1)S(1)}, u32[]{:S(2)}, u32[]{:S(2)}) collective-permute-start(bf16[4,80,640]{2,1,0:T(8,128)(2,1)S(1)} %get-tuple-element.60), channel_id=1, source_target_pairs={{0,32},{4,36},{8,40},{12,44},{16,48},{20,52},{24,56},{28,60},{32,6... | collective-permute-start | bytes 1228808 | tf_op jit(solution)/shard_map/ppermute | solution.py:27
  158.3 29.6 %collective-permute-start.23 = (bf16[512,640]{1,0:T(8,128)(2,1)S(1)}, bf16[512,640]{1,0:T(8,128)(2,1)S(1)}, u32[]{:S(2)}, u32[]{:S(2)}) collective-permute-start(bf16[512,640]{1,0:T(8,128)(2,1)S(1)} %fusion.32), channel_id=1, source_target_pairs={{0,1},{1,2},{2,3},{3,0},{4,5},{5,6},{6,7},{7,4},{8,9},{9,10},{10,1... | collective-permute-start | bytes 1966088 | tf_op jit(solution)/shard_map/ppermute | solution.py:39
  158.4 29.5 %collective-permute-start.24 = (bf16[512,640]{1,0:T(8,128)(2,1)S(1)}, bf16[512,640]{1,0:T(8,128)(2,1)S(1)}, u32[]{:S(2)}, u32[]{:S(2)}) collective-permute-start(bf16[512,640]{1,0:T(8,128)(2,1)S(1)} %fusion.35), channel_id=1, source_target_pairs={{0,3},{1,0},{2,1},{3,2},{4,7},{5,4},{6,5},{7,6},{8,11},{9,8},{10,9... | collective-permute-start | bytes 1966088 | tf_op jit(solution)/shard_map/ppermute | solution.py:39
  167.5 6.2 %collective-permute-start.22 = (bf16[80,640]{1,0:T(8,128)(2,1)S(1)}, bf16[80,640]{1,0:T(8,128)(2,1)S(1)}, u32[]{:S(2)}, u32[]{:S(2)}) collective-permute-start(bf16[80,640]{1,0:T(8,128)(2,1)S(1)} %get-tuple-element.63), channel_id=1, source_target_pairs={{0,64},{4,68},{8,72},{12,76},{16,80},{20,84},{24,88},{28,92},{32,9... | collective-permute-start | bytes 307208 | tf_op jit(solution)/shard_map/ppermute | solution.py:27
  169.2 6.8 %collective-permute-start.21 = (bf16[80,640]{1,0:T(8,128)(2,1)S(1)}, bf16[80,640]{1,0:T(8,128)(2,1)S(1)}, u32[]{:S(2)}, u32[]{:S(2)}) collective-permute-start(bf16[80,640]{1,0:T(8,128)(2,1)S(1)} %get-tuple-element.64), channel_id=1, source_target_pairs={{0,96},{4,100},{8,104},{12,108},{16,112},{20,116},{24,120},{28,124... | collective-permute-start | bytes 307208 | tf_op jit(solution)/shard_map/ppermute | solution.py:27
  170.3 8.3 %collective-permute-start.20 = (bf16[80,640]{1,0:T(8,128)(2,1)S(1)}, bf16[80,640]{1,0:T(8,128)(2,1)S(1)}, u32[]{:S(2)}, u32[]{:S(2)}) collective-permute-start(bf16[80,640]{1,0:T(8,128)(2,1)S(1)} %get-tuple-element.65), channel_id=1, source_target_pairs={{0,32},{4,36},{8,40},{12,44},{16,48},{20,52},{24,56},{28,60},{32,6... | collective-permute-start | bytes 307208 | tf_op jit(solution)/shard_map/ppermute | solution.py:27
  173.7 7.2 %collective-permute-start.19 = (bf16[80,640]{1,0:T(8,128)(2,1)S(1)}, bf16[80,640]{1,0:T(8,128)(2,1)S(1)}, u32[]{:S(2)}, u32[]{:S(2)}) collective-permute-start(bf16[80,640]{1,0:T(8,128)(2,1)S(1)} %get-tuple-element.66), channel_id=1, source_target_pairs={{0,16},{4,20},{8,24},{12,28},{16,0},{20,4},{24,8},{28,12},{32,48},... | collective-permute-start | bytes 307208 | tf_op jit(solution)/shard_map/ppermute | solution.py:33
  178.6 5.9 %collective-permute-start.17 = (bf16[80,640]{1,0:T(8,128)(2,1)S(1)}, bf16[80,640]{1,0:T(8,128)(2,1)S(1)}, u32[]{:S(2)}, u32[]{:S(2)}) collective-permute-start(bf16[80,640]{1,0:T(8,128)(2,1)S(1)} %get-tuple-element.68), channel_id=1, source_target_pairs={{0,8},{4,12},{8,16},{12,20},{16,24},{20,28},{24,0},{28,4},{32,40},... | collective-permute-start | bytes 307208 | tf_op jit(solution)/shard_map/ppermute | solution.py:33
  184.6 11.6 %collective-permute-start.25 = (bf16[160,640]{1,0:T(8,128)(2,1)S(1)}, bf16[160,640]{1,0:T(8,128)(2,1)S(1)}, u32[]{:S(2)}, u32[]{:S(2)}) collective-permute-start(bf16[160,640]{1,0:T(8,128)(2,1)S(1)} %fusion.44), channel_id=1, source_target_pairs={{0,0},{1,32},{2,64},{3,96},{4,4},{5,36},{6,68},{7,100},{8,8},{9,40... | collective-permute-start | bytes 614408 | tf_op jit(solution)/shard_map/ppermute | solution.py:52
  (21 other events, 147.3 us)
Sparse Core Ops, SparseCore 0:
  71.1 49.3 all-gather.1

commit v4 on v3

--- a/solution.py
+++ b/solution.py
@@ -335,9 +335,7 @@
     weight = lax.all_gather(weight_tile, "dp", axis=0, tiled=True)
     weight = weight.reshape(NX, -1, feat_width)
 
-    below, above = along_y(acts, 1), along_y(acts, 3)
-    middle = tokens // 2
-    far = jnp.concatenate([along_y(below[:middle], 1), along_y(above[middle:], 3)], axis=0)
+    below, far, above = [along_y(acts, s) for s in (1, 2, 3)]
     mine = [acts, below, far, above]
     theirs = [to_partner(block_cols) for block_cols in mine]
 

time: 205 us -> 205 us (level)
  waiting for transfers between devices: 58.3 us -> 66.6 us
  starting transfers between devices: 48.4 us -> 40.8 us
  local copies, waits for them, and re-layouts: 12.7 us -> 10.2 us
  matrix products: 13.7 us -> 16 us
    ppermute x7 -> x6, waiting for transfers between devices: 15.4 us -> 20.8 us  [along_y(): return lax.ppermute(value, 'mp', [(y, (y + shift) % NY) for y in range(NY)])]
    ppermute x6, starting transfers between devices: 12 us -> 6.9 us  [along_x(): lax.ppermute(value, 'dp', [(place(x, z, c), place(x + shift, z, c)) for x...]
    ppermute x7 -> x6, starting transfers between devices: 10 us -> 6.75 us  [along_y(): return lax.ppermute(value, 'mp', [(y, (y + shift) % NY) for y in range(NY)])]
    dot_general x4, matrix products: 5.98 us -> 8.23 us  [local(): lax.dot_general(mine[s], columns(y - s + NY), (((1,), (1,)), ((), ())), p...]
  transfers between devices with their start and end apart: 28 -> 27, of which waited for: 10 -> 12; matrix products, arithmetic and copies ran while one was open for 14% -> 13% of each run, Pallas kernels for 13% -> 13%
where the time goes in v4:
time: 205 us; the launch traced here: 204 us
  waiting for transfers between devices  66.6 us (32%)
  Pallas kernels  50.3 us (25%)
  starting transfers between devices  40.8 us (20%)
  matrix products  16 us (8%)
  between operations  14.3 us (7%)
  local copies, waits for them, and re-layouts  10.2 us (5%)
  other arithmetic  5.96 us (3%)
    ppermute x2, waiting for transfers between devices, swap_xy(): return lax.ppermute(value, ('dp', 'mp'), pairs)  32.4 us
    ppermute x6, waiting for transfers between devices, along_y(): return lax.ppermute(value, 'mp', [(y, (y + shift) % NY) for y in range(NY)])  20.8 us
    pallas_call x2, Pallas kernels, attend(): pl.pallas_call(functools.partial(attend_kernel, first=first), out_shape=j...  19.7 us
    pallas_call x2, Pallas kernels, grad_parts(): pl.pallas_call(functools.partial(grad_kernel, shifts=shifts, kept=kept),...  13.4 us
    ppermute x2, starting transfers between devices, swap_xy(): return lax.ppermute(value, ('dp', 'mp'), pairs)  9.38 us
    all_to_all x1, starting transfers between devices, local(): lax.all_to_all(send_rows, 'dp', split_axis=0, concat_axis=0, tiled=True)  8.58 us
    ppermute x6, starting transfers between devices, along_z(): lax.ppermute(value, 'dp', [(place(x, z, c), place(x, z + shift, c)) for x...  8.52 us
    dot_general x4, matrix products, local(): lax.dot_general(mine[s], columns(y - s + NY), (((1,), (1,)), ((), ())), p...  8.23 us
  transfers between devices with their start and end apart: 27, of which 12 were waited for; matrix products, arithmetic and copies ran while one was open for 13% of the time, Pallas kernels for 13%

profile of v4, /device:TPU:4, one launch (start us, length us, event | category | flops | bytes accessed | tf_op | source)
XLA Modules:
  0.0 204.2 jit_solution(3177604012262844813)
XLA Ops:
  7.2 9.8 %attend.3.b_ref = bf16[256,640]{1,0:T(8,128)(2,1)} custom-call(s32[128]{0:T(128)} %lengths_ref.3, bf16[128,4,640]{2,1,0:T(4,128)(2,1)} %q_ref.3, bf16[512,128]{1,0:T(8,128)(2,1)} %bitcast.107, bf16[512,128]{1,0:T(8,128)(2,1)} %bitcast.109, bf16[128,256,128]{2,1,0:T(8,128)(2,1)} %k_ref.3, bf16[128,256,128]{2,1,0:T(8,128)(2,1)} %v_ref.3), custom_call_target="tpu_custom_call" | custom-call | tf_op jit(solution)/shard_map/attend/pallas_call | solution.py:116
  17.0 9.9 %attend.2.a_ref = bf16[256,640]{1,0:T(8,128)(2,1)} custom-call(s32[128]{0:T(128)} %lengths_ref.3, bf16[128,4,640]{2,1,0:T(4,128)(2,1)} %q_ref.3, bf16[512,128]{1,0:T(8,128)(2,1)} %bitcast.108, bf16[512,128]{1,0:T(8,128)(2,1)} %bitcast.110, bf16[128,256,128]{2,1,0:T(8,128)(2,1)} %k_ref.3, bf16[128,256,128]{2,1,0:T(8,128)(2,1)} %v_ref.3), custom_call_target="tpu_custom_call" | custom-call | tf_op jit(solution)/shard_map/attend/pallas_call | solution.py:116
  28.5 3.8 %pack.1 = bf16[32,40,640]{2,1,0:T(8,128)(2,1)} custom-call(s32[1,512]{1,0:T(1,128)} %add.177.goes_ref, bf16[8,640]{1,0:T(8,128)(2,1)} %convert_convert_fusion.facts_ref, bf16[256,640]{1,0:T(8,128)(2,1)} %attend.2.a_ref, bf16[256,640]{1,0:T(8,128)(2,1)} %attend.3.b_ref), custom_call_target="tpu_custom_call" | custom-call | tf_op jit(solution)/shard_map/pack/pallas_call | solution.py:153
  32.3 8.6 %all-to-all-start = ((bf16[32,40,640]{2,1,0:T(8,128)(2,1)}), bf16[32,40,640]{2,1,0:T(8,128)(2,1)S(1)}, u32[]{:S(2)}, u32[]{:S(2)}) async-start(bf16[32,40,640]{2,1,0:T(8,128)(2,1)} %pack.1), calls=%async_computation | async-start | bytes 3276800 | tf_op jit(solution)/shard_map/all_to_all | solution.py:331
  40.9 4.8 %collective-permute-start.14 = (bf16[160,640]{1,0:T(8,128)(2,1)S(1)}, bf16[160,640]{1,0:T(8,128)(2,1)S(1)}, u32[]{:S(2)}, u32[]{:S(2)}) collective-permute-start(bf16[160,640]{1,0:T(8,128)(2,1)S(1)} %copy-done.12), channel_id=1, source_target_pairs={{0,0},{1,32},{2,64},{3,96},{4,4},{5,36},{6,68},{7,100},{8,8},{9,40... | collective-permute-start | bytes 614408 | tf_op jit(solution)/shard_map/ppermute | solution.py:52
  45.7 24.5 %collective-permute-done.14 = bf16[160,640]{1,0:T(8,128)(2,1)S(1)} collective-permute-done((bf16[160,640]{1,0:T(8,128)(2,1)S(1)}, bf16[160,640]{1,0:T(8,128)(2,1)S(1)}, u32[]{:S(2)}, u32[]{:S(2)}) %collective-permute-start.14) | collective-permute-done | bytes 204832 | tf_op jit(solution)/shard_map/ppermute | solution.py:52
  71.6 5.6 %unpack.1 = (bf16[512,640]{1,0:T(8,128)(2,1)}, s32[512,1]{1,0:T(8,128)}) custom-call(s32[1]{0:T(128)} %bitcast.11.block_ref, bf16[32,40,640]{2,1,0:T(8,128)(2,1)} %copy-done, bf16[1280,640]{1,0:T(8,128)(2,1)} %bitcast.103), custom_call_target="tpu_custom_call" | custom-call | tf_op jit(solution)/shard_map/unpack/pallas_call | solution.py:187
  80.5 7.8 %weigh.1 = bf16[512,1280]{1,0:T(8,128)(2,1)} custom-call(bf16[32,40,640]{2,1,0:T(8,128)(2,1)} %copy-done, s32[512,1]{1,0:T(8,128)} %get-tuple-element.29.word_ref, bf16[512,1280]{1,0:T(8,128)(2,1)} %cot_ref.1), custom_call_target="tpu_custom_call" | custom-call | tf_op jit(solution)/shard_map/weigh/pallas_call | solution.py:229
  91.4 15.4 %collective-permute-done.4.refs_2_ = bf16[512,640]{1,0:T(8,128)(2,1)} collective-permute-done((bf16[512,640]{1,0:T(8,128)(2,1)}, bf16[512,640]{1,0:T(8,128)(2,1)}, u32[]{:S(2)}, u32[]{:S(2)}) %collective-permute-start.4) | collective-permute-done | bytes 655392 | tf_op jit(solution)/shard_map/ppermute | solution.py:39
  106.9 3.4 %collective-permute-done.3.refs_1_ = bf16[512,640]{1,0:T(8,128)(2,1)} collective-permute-done((bf16[512,640]{1,0:T(8,128)(2,1)}, bf16[512,640]{1,0:T(8,128)(2,1)}, u32[]{:S(2)}, u32[]{:S(2)}) %collective-permute-start.3) | collective-permute-done | bytes 655392 | tf_op jit(solution)/shard_map/ppermute | solution.py:39
  112.7 7.7 %grad_parts.2 = (bf16[4,4,80,640]{3,2,1,0:T(8,128)(2,1)}, bf16[4,4,80,640]{3,2,1,0:T(8,128)(2,1)}) custom-call(s32[3]{0:T(128)} %pad_add_fusion.where_ref, bf16[640,1024]{1,0:T(8,128)(2,1)} %pad_maximum_fusion.left_ref, bf16[512,640]{1,0:T(8,128)(2,1)} %get-tuple-element.43.refs_0_, bf16[512,640]{1,0:T(8,128)(2,1)} %collective-permute-done.3.refs_1_, ...), custom_call_target="tpu_custom_call" | custom-call | tf_op jit(solution)/shard_map/grad_parts/pallas_call | solution.py:272
  121.3 5.7 %grad_parts.3 = (bf16[4,4,80,640]{3,2,1,0:T(8,128)(2,1)}, bf16[4,4,80,640]{3,2,1,0:T(8,128)(2,1)}) custom-call(s32[3]{0:T(128)} %pad_add_fusion.where_ref, bf16[640,1024]{1,0:T(8,128)(2,1)} %pad_maximum_fusion.left_ref, bf16[512,640]{1,0:T(8,128)(2,1)} %copy-done.5, bf16[512,640]{1,0:T(8,128)(2,1)} %copy-done.7, ...), custom_call_target="tpu_custom_call" | custom-call | tf_op jit(solution)/shard_map/grad_parts/pallas_call | solution.py:272
  127.0 2.5 %slice_bitcast_fusion = (bf16[4,80,640]{2,1,0:T(8,128)(2,1)}, bf16[4,80,640]{2,1,0:T(8,128)(2,1)}, bf16[4,80,640]{2,1,0:T(8,128)(2,1)}) fusion(bf16[4,4,80,640]{3,2,1,0:T(8,128)(2,1)} %get-tuple-element.34), kind=kLoop, calls=%fused_computation.45 | loop fusion | bytes 2457600 | tf_op jit(solution)/shard_map/squeeze | solution.py:354
  129.5 2.8 %collective-permute-start.13 = (bf16[4,80,640]{2,1,0:T(8,128)(2,1)}, bf16[4,80,640]{2,1,0:T(8,128)(2,1)}, u32[]{:S(2)}, u32[]{:S(2)}) collective-permute-start(bf16[4,80,640]{2,1,0:T(8,128)(2,1)} %get-tuple-element.55), channel_id=1, source_target_pairs={{0,16},{4,20},{8,24},{12,28},{16,0},{20,4},{24,8},{28,12},{32,48},... | collective-permute-start | bytes 1228808 | tf_op jit(solution)/shard_map/ppermute | solution.py:33
  135.5 2.6 %collective-permute-start.10 = (bf16[4,80,640]{2,1,0:T(8,128)(2,1)}, bf16[4,80,640]{2,1,0:T(8,128)(2,1)}, u32[]{:S(2)}, u32[]{:S(2)}) collective-permute-start(bf16[4,80,640]{2,1,0:T(8,128)(2,1)} %get-tuple-element.58), channel_id=1, source_target_pairs={{0,64},{4,68},{8,72},{12,76},{16,80},{20,84},{24,88},{28,92},{32,9... | collective-permute-start | bytes 1228808 | tf_op jit(solution)/shard_map/ppermute | solution.py:27
  138.1 2.8 %fusion.29 = bf16[512,640]{1,0:T(8,128)(2,1)S(1)} fusion(bf16[512,1280]{1,0:T(8,128)(2,1)S(1)} %copy-done.1, bf16[4,1280,640]{2,1,0:T(8,128)(2,1)} %bitcast.111, s32[]{:T(128)S(6)} %select_n.101), kind=kOutput, calls=%fused_computation.28 | convolution fusion | flops 839188480 | bytes 3604484 | tf_op jit(solution)/shard_map/dot_general | solution.py:361
  140.9 2.6 %fusion.35 = bf16[512,640]{1,0:T(8,128)(2,1)S(1)} fusion(bf16[512,1280]{1,0:T(8,128)(2,1)S(1)} %copy-done.1, bf16[4,1280,640]{2,1,0:T(8,128)(2,1)} %bitcast.112, s32[]{:T(128)S(6)} %select_n.105), kind=kOutput, calls=%fused_computation.30 | convolution fusion | flops 839188480 | bytes 3604484 | tf_op jit(solution)/shard_map/dot_general | solution.py:361
  149.7 2.9 %collective-permute-done.12 = bf16[4,80,640]{2,1,0:T(8,128)(2,1)} collective-permute-done((bf16[4,80,640]{2,1,0:T(8,128)(2,1)}, bf16[4,80,640]{2,1,0:T(8,128)(2,1)}, u32[]{:S(2)}, u32[]{:S(2)}) %collective-permute-start.12) | collective-permute-done | bytes 409632 | tf_op jit(solution)/shard_map/ppermute | solution.py:33
  159.5 3.7 %collective-permute-done.8 = bf16[4,80,640]{2,1,0:T(8,128)(2,1)S(1)} collective-permute-done((bf16[4,80,640]{2,1,0:T(8,128)(2,1)S(1)}, bf16[4,80,640]{2,1,0:T(8,128)(2,1)S(1)}, u32[]{:S(2)}, u32[]{:S(2)}) %collective-permute-start.8) | collective-permute-done | bytes 409632 | tf_op jit(solution)/shard_map/ppermute | solution.py:27
  170.2 3.2 %collective-permute-done.21 = bf16[80,640]{1,0:T(8,128)(2,1)S(1)} collective-permute-done((bf16[80,640]{1,0:T(8,128)(2,1)S(1)}, bf16[80,640]{1,0:T(8,128)(2,1)S(1)}, u32[]{:S(2)}, u32[]{:S(2)}) %collective-permute-start.21) | collective-permute-done | bytes 102432 | tf_op jit(solution)/shard_map/ppermute | solution.py:27
  174.0 2.9 %collective-permute-start.17 = (bf16[80,640]{1,0:T(8,128)(2,1)S(1)}, bf16[80,640]{1,0:T(8,128)(2,1)S(1)}, u32[]{:S(2)}, u32[]{:S(2)}) collective-permute-start(bf16[80,640]{1,0:T(8,128)(2,1)S(1)} %get-tuple-element.67), channel_id=1, source_target_pairs={{0,24},{4,28},{8,0},{12,4},{16,8},{20,12},{24,16},{28,20},{32,56},... | collective-permute-start | bytes 307208 | tf_op jit(solution)/shard_map/ppermute | solution.py:33
  180.3 2.5 %collective-permute-done.16 = bf16[80,640]{1,0:T(8,128)(2,1)S(1)} collective-permute-done((bf16[80,640]{1,0:T(8,128)(2,1)S(1)}, bf16[80,640]{1,0:T(8,128)(2,1)S(1)}, u32[]{:S(2)}, u32[]{:S(2)}) %collective-permute-start.16) | collective-permute-done | bytes 102432 | tf_op jit(solution)/shard_map/ppermute | solution.py:33
  183.0 4.6 %collective-permute-start.24 = (bf16[160,640]{1,0:T(8,128)(2,1)S(1)}, bf16[160,640]{1,0:T(8,128)(2,1)S(1)}, u32[]{:S(2)}, u32[]{:S(2)}) collective-permute-start(bf16[160,640]{1,0:T(8,128)(2,1)S(1)} %fusion.44), channel_id=1, source_target_pairs={{0,0},{1,32},{2,64},{3,96},{4,4},{5,36},{6,68},{7,100},{8,8},{9,40... | collective-permute-start | bytes 614408 | tf_op jit(solution)/shard_map/ppermute | solution.py:52
  188.8 7.9 %collective-permute-done.24 = bf16[160,640]{1,0:T(8,128)(2,1)S(1)} collective-permute-done((bf16[160,640]{1,0:T(8,128)(2,1)S(1)}, bf16[160,640]{1,0:T(8,128)(2,1)S(1)}, u32[]{:S(2)}, u32[]{:S(2)}) %collective-permute-start.24) | collective-permute-done | bytes 204832 | tf_op jit(solution)/shard_map/ppermute | solution.py:52
  (99 shorter events, 41.8 us)
Async XLA Ops:
  32.3 37.9 %all-to-all-start = ((bf16[32,40,640]{2,1,0:T(8,128)(2,1)}), bf16[32,40,640]{2,1,0:T(8,128)(2,1)S(1)}, u32[]{:S(2)}, u32[]{:S(2)}) async-start(bf16[32,40,640]{2,1,0:T(8,128)(2,1)} %pack.1), calls=%async_computation | async-start | bytes 3276800 | tf_op jit(solution)/shard_map/all_to_all | solution.py:331
  40.9 97.2 %all-gather.2.cloned.1.call-start = ((), (), s32[]{:S(2)}) async-start(), calls=%async_computation.1 | async-start | bytes 6758400 | tf_op jit(solution)/shard_map/all_gather | solution.py:335
  40.9 29.3 %collective-permute-start.14 = (bf16[160,640]{1,0:T(8,128)(2,1)S(1)}, bf16[160,640]{1,0:T(8,128)(2,1)S(1)}, u32[]{:S(2)}, u32[]{:S(2)}) collective-permute-start(bf16[160,640]{1,0:T(8,128)(2,1)S(1)} %copy-done.12), channel_id=1, source_target_pairs={{0,0},{1,32},{2,64},{3,96},{4,4},{5,36},{6,68},{7,100},{8,8},{9,40... | collective-permute-start | bytes 614408 | tf_op jit(solution)/shard_map/ppermute | solution.py:52
  77.2 29.7 %collective-permute-start.4 = (bf16[512,640]{1,0:T(8,128)(2,1)}, bf16[512,640]{1,0:T(8,128)(2,1)}, u32[]{:S(2)}, u32[]{:S(2)}) collective-permute-start(bf16[512,640]{1,0:T(8,128)(2,1)} %get-tuple-element.43.refs_0_), channel_id=1, source_target_pairs={{0,3},{1,0},{2,1},{3,2},{4,7},{5,4},{6,5},{7,6},{8,11},{9,8},{10,9... | collective-permute-start | bytes 1966088 | tf_op jit(solution)/shard_map/ppermute | solution.py:39
  79.0 31.3 %collective-permute-start.3 = (bf16[512,640]{1,0:T(8,128)(2,1)}, bf16[512,640]{1,0:T(8,128)(2,1)}, u32[]{:S(2)}, u32[]{:S(2)}) collective-permute-start(bf16[512,640]{1,0:T(8,128)(2,1)} %get-tuple-element.43.refs_0_), channel_id=1, source_target_pairs={{0,1},{1,2},{2,3},{3,0},{4,5},{5,6},{6,7},{7,4},{8,9},{9,10},{10,1... | collective-permute-start | bytes 1966088 | tf_op jit(solution)/shard_map/ppermute | solution.py:39
  79.2 31.1 %collective-permute-start.1 = (bf16[512,640]{1,0:T(8,128)(2,1)}, bf16[512,640]{1,0:T(8,128)(2,1)S(1)}, u32[]{:S(2)}, u32[]{:S(2)}) collective-permute-start(bf16[512,640]{1,0:T(8,128)(2,1)} %get-tuple-element.43.refs_0_), channel_id=1, source_target_pairs={{0,2},{1,3},{2,0},{3,1},{4,6},{5,7},{6,4},{7,5},{8,10},{9,11},{10,... | collective-permute-start | bytes 1966088 | tf_op jit(solution)/shard_map/ppermute | solution.py:39
  90.9 20.5 %collective-permute-start = (bf16[640,512]{1,0:T(8,128)(2,1)}, bf16[640,512]{1,0:T(8,128)(2,1)S(1)}, u32[]{:S(2)}, u32[]{:S(2)}) collective-permute-start(bf16[640,512]{1,0:T(8,128)(2,1)} %get-tuple-element.62), channel_id=1, source_target_pairs={{0,4},{4,0},{8,12},{12,8},{16,20},{20,16},{24,28},{28,24},{32,36},... | collective-permute-start | bytes 1966088 | tf_op jit(solution)/shard_map/ppermute | solution.py:43
  91.3 21.3 %collective-permute-start.5 = (bf16[512,640]{1,0:T(8,128)(2,1)S(1)}, bf16[512,640]{1,0:T(8,128)(2,1)}, u32[]{:S(2)}, u32[]{:S(2)}) collective-permute-start(bf16[512,640]{1,0:T(8,128)(2,1)S(1)} %copy-done.2), channel_id=1, source_target_pairs={{0,4},{4,0},{8,12},{12,8},{16,20},{20,16},{24,28},{28,24},{32,36},... | collective-permute-start | bytes 1966088 | tf_op jit(solution)/shard_map/ppermute | solution.py:43
  110.3 10.2 %collective-permute-start.2 = (bf16[512,640]{1,0:T(8,128)(2,1)S(1)}, bf16[512,640]{1,0:T(8,128)(2,1)S(1)}, u32[]{:S(2)}, u32[]{:S(2)}) collective-permute-start(bf16[512,640]{1,0:T(8,128)(2,1)S(1)} %collective-permute-done.1.refs_0_), channel_id=1, source_target_pairs={{0,4},{4,0},{8,12},{12,8},{16,20},{20,16},{24,28},{28,24},{32,36},... | collective-permute-start | bytes 1966088 | tf_op jit(solution)/shard_map/ppermute | solution.py:43
  129.5 18.9 %collective-permute-start.13 = (bf16[4,80,640]{2,1,0:T(8,128)(2,1)}, bf16[4,80,640]{2,1,0:T(8,128)(2,1)}, u32[]{:S(2)}, u32[]{:S(2)}) collective-permute-start(bf16[4,80,640]{2,1,0:T(8,128)(2,1)} %get-tuple-element.55), channel_id=1, source_target_pairs={{0,16},{4,20},{8,24},{12,28},{16,0},{20,4},{24,8},{28,12},{32,48},... | collective-permute-start | bytes 1228808 | tf_op jit(solution)/shard_map/ppermute | solution.py:33
  132.3 20.3 %collective-permute-start.12 = (bf16[4,80,640]{2,1,0:T(8,128)(2,1)}, bf16[4,80,640]{2,1,0:T(8,128)(2,1)}, u32[]{:S(2)}, u32[]{:S(2)}) collective-permute-start(bf16[4,80,640]{2,1,0:T(8,128)(2,1)} %get-tuple-element.56), channel_id=1, source_target_pairs={{0,24},{4,28},{8,0},{12,4},{16,8},{20,12},{24,16},{28,20},{32,56},... | collective-permute-start | bytes 1228808 | tf_op jit(solution)/shard_map/ppermute | solution.py:33
  134.5 21.7 %collective-permute-start.11 = (bf16[4,80,640]{2,1,0:T(8,128)(2,1)}, bf16[4,80,640]{2,1,0:T(8,128)(2,1)}, u32[]{:S(2)}, u32[]{:S(2)}) collective-permute-start(bf16[4,80,640]{2,1,0:T(8,128)(2,1)} %get-tuple-element.57), channel_id=1, source_target_pairs={{0,8},{4,12},{8,16},{12,20},{16,24},{20,28},{24,0},{28,4},{32,40},... | collective-permute-start | bytes 1228808 | tf_op jit(solution)/shard_map/ppermute | solution.py:33
  135.5 21.8 %collective-permute-start.10 = (bf16[4,80,640]{2,1,0:T(8,128)(2,1)}, bf16[4,80,640]{2,1,0:T(8,128)(2,1)}, u32[]{:S(2)}, u32[]{:S(2)}) collective-permute-start(bf16[4,80,640]{2,1,0:T(8,128)(2,1)} %get-tuple-element.58), channel_id=1, source_target_pairs={{0,64},{4,68},{8,72},{12,76},{16,80},{20,84},{24,88},{28,92},{32,9... | collective-permute-start | bytes 1228808 | tf_op jit(solution)/shard_map/ppermute | solution.py:27
  145.9 19.3 %collective-permute-start.15 = (bf16[512,640]{1,0:T(8,128)(2,1)S(1)}, bf16[512,640]{1,0:T(8,128)(2,1)S(1)}, u32[]{:S(2)}, u32[]{:S(2)}) collective-permute-start(bf16[512,640]{1,0:T(8,128)(2,1)S(1)} %fusion.26), channel_id=1, source_target_pairs={{0,2},{1,3},{2,0},{3,1},{4,6},{5,7},{6,4},{7,5},{8,10},{9,11},{10,... | collective-permute-start | bytes 1966088 | tf_op jit(solution)/shard_map/ppermute | solution.py:39
  148.4 11.1 %collective-permute-start.9 = (bf16[4,80,640]{2,1,0:T(8,128)(2,1)S(1)}, bf16[4,80,640]{2,1,0:T(8,128)(2,1)S(1)}, u32[]{:S(2)}, u32[]{:S(2)}) collective-permute-start(bf16[4,80,640]{2,1,0:T(8,128)(2,1)S(1)} %copy-done.8), channel_id=1, source_target_pairs={{0,96},{4,100},{8,104},{12,108},{16,112},{20,116},{24,120},{28,124... | collective-permute-start | bytes 1228808 | tf_op jit(solution)/shard_map/ppermute | solution.py:27
  152.7 10.6 %collective-permute-start.8 = (bf16[4,80,640]{2,1,0:T(8,128)(2,1)S(1)}, bf16[4,80,640]{2,1,0:T(8,128)(2,1)S(1)}, u32[]{:S(2)}, u32[]{:S(2)}) collective-permute-start(bf16[4,80,640]{2,1,0:T(8,128)(2,1)S(1)} %get-tuple-element.60), channel_id=1, source_target_pairs={{0,32},{4,36},{8,40},{12,44},{16,48},{20,52},{24,56},{28,60},{32,6... | collective-permute-start | bytes 1228808 | tf_op jit(solution)/shard_map/ppermute | solution.py:27
  156.2 31.4 %collective-permute-start.22 = (bf16[512,640]{1,0:T(8,128)(2,1)S(1)}, bf16[512,640]{1,0:T(8,128)(2,1)S(1)}, u32[]{:S(2)}, u32[]{:S(2)}) collective-permute-start(bf16[512,640]{1,0:T(8,128)(2,1)S(1)} %fusion.32), channel_id=1, source_target_pairs={{0,1},{1,2},{2,3},{3,0},{4,5},{5,6},{6,7},{7,4},{8,9},{9,10},{10,1... | collective-permute-start | bytes 1966088 | tf_op jit(solution)/shard_map/ppermute | solution.py:39
  157.3 30.3 %collective-permute-start.23 = (bf16[512,640]{1,0:T(8,128)(2,1)S(1)}, bf16[512,640]{1,0:T(8,128)(2,1)S(1)}, u32[]{:S(2)}, u32[]{:S(2)}) collective-permute-start(bf16[512,640]{1,0:T(8,128)(2,1)S(1)} %fusion.35), channel_id=1, source_target_pairs={{0,3},{1,0},{2,1},{3,2},{4,7},{5,4},{6,5},{7,6},{8,11},{9,8},{10,9... | collective-permute-start | bytes 1966088 | tf_op jit(solution)/shard_map/ppermute | solution.py:39
  167.1 6.3 %collective-permute-start.21 = (bf16[80,640]{1,0:T(8,128)(2,1)S(1)}, bf16[80,640]{1,0:T(8,128)(2,1)S(1)}, u32[]{:S(2)}, u32[]{:S(2)}) collective-permute-start(bf16[80,640]{1,0:T(8,128)(2,1)S(1)} %get-tuple-element.63), channel_id=1, source_target_pairs={{0,64},{4,68},{8,72},{12,76},{16,80},{20,84},{24,88},{28,92},{32,9... | collective-permute-start | bytes 307208 | tf_op jit(solution)/shard_map/ppermute | solution.py:27
  168.2 8.8 %collective-permute-start.19 = (bf16[80,640]{1,0:T(8,128)(2,1)S(1)}, bf16[80,640]{1,0:T(8,128)(2,1)S(1)}, u32[]{:S(2)}, u32[]{:S(2)}) collective-permute-start(bf16[80,640]{1,0:T(8,128)(2,1)S(1)} %get-tuple-element.65), channel_id=1, source_target_pairs={{0,32},{4,36},{8,40},{12,44},{16,48},{20,52},{24,56},{28,60},{32,6... | collective-permute-start | bytes 307208 | tf_op jit(solution)/shard_map/ppermute | solution.py:27
  173.4 6.3 %collective-permute-start.18 = (bf16[80,640]{1,0:T(8,128)(2,1)S(1)}, bf16[80,640]{1,0:T(8,128)(2,1)S(1)}, u32[]{:S(2)}, u32[]{:S(2)}) collective-permute-start(bf16[80,640]{1,0:T(8,128)(2,1)S(1)} %get-tuple-element.66), channel_id=1, source_target_pairs={{0,16},{4,20},{8,24},{12,28},{16,0},{20,4},{24,8},{28,12},{32,48},... | collective-permute-start | bytes 307208 | tf_op jit(solution)/shard_map/ppermute | solution.py:33
  174.0 6.3 %collective-permute-start.17 = (bf16[80,640]{1,0:T(8,128)(2,1)S(1)}, bf16[80,640]{1,0:T(8,128)(2,1)S(1)}, u32[]{:S(2)}, u32[]{:S(2)}) collective-permute-start(bf16[80,640]{1,0:T(8,128)(2,1)S(1)} %get-tuple-element.67), channel_id=1, source_target_pairs={{0,24},{4,28},{8,0},{12,4},{16,8},{20,12},{24,16},{28,20},{32,56},... | collective-permute-start | bytes 307208 | tf_op jit(solution)/shard_map/ppermute | solution.py:33
  176.9 5.9 %collective-permute-start.16 = (bf16[80,640]{1,0:T(8,128)(2,1)S(1)}, bf16[80,640]{1,0:T(8,128)(2,1)S(1)}, u32[]{:S(2)}, u32[]{:S(2)}) collective-permute-start(bf16[80,640]{1,0:T(8,128)(2,1)S(1)} %get-tuple-element.68), channel_id=1, source_target_pairs={{0,8},{4,12},{8,16},{12,20},{16,24},{20,28},{24,0},{28,4},{32,40},... | collective-permute-start | bytes 307208 | tf_op jit(solution)/shard_map/ppermute | solution.py:33
  183.0 13.7 %collective-permute-start.24 = (bf16[160,640]{1,0:T(8,128)(2,1)S(1)}, bf16[160,640]{1,0:T(8,128)(2,1)S(1)}, u32[]{:S(2)}, u32[]{:S(2)}) collective-permute-start(bf16[160,640]{1,0:T(8,128)(2,1)S(1)} %fusion.44), channel_id=1, source_target_pairs={{0,0},{1,32},{2,64},{3,96},{4,4},{5,36},{6,68},{7,100},{8,8},{9,40... | collective-permute-start | bytes 614408 | tf_op jit(solution)/shard_map/ppermute | solution.py:52
  (18 other events, 107.9 us)
Sparse Core Ops, SparseCore 0:
  71.1 49.3 all-gather.1
